TPU v7x, 32 devices: a whole 2x2x4 slice. The times are simulated.
32 devices in a mesh: group: 2 (over y), replica: 16 (over z, x, core).
Axes of the slice: x: 2, y: 2, z: 4, core: 2. Of those that a mesh axis runs over, the one named last changes fastest.
Arguments:
- tokens: bfloat16 [32, 144, 896], P(('group', 'replica')), may hold values from -6 to 6
- segments: int32 [32, 144], P(('group', 'replica')), may hold values from 0 to 35, never falling along the last dimension, each value on 1 to 72 neighbouring positions
- norm1_gain: bfloat16 [896], P('group'), may hold values from 0.5 to 1.5
- qkv_weight: bfloat16 [896, 1152], P('group'), may hold values from -0.1875 to 0.1875
- qkv_bias: bfloat16 [1152], P('group'), may hold values from -2.5 to 2.5
- out_weight: bfloat16 [896, 896], P('group'), may hold values from -0.375 to 0.375
- norm2_gain: bfloat16 [896], P('group'), may hold values from 0.5 to 1.5
- gate_weight: bfloat16 [896, 4864], P(None, 'group'), may hold values from -0.1875 to 0.1875
- up_weight: bfloat16 [896, 4864], P(None, 'group'), may hold values from -0.1875 to 0.1875
- down_weight: bfloat16 [4864, 896], P('group'), may hold values from -0.078125 to 0.078125
- cotangent: bfloat16 [32, 144, 896], P(('group', 'replica')), may hold values from -6 to 6
Outputs:
- result: float32 [32, 144, 896], P(('group', 'replica'))
- back_tokens: float32 [32, 144, 896], P(('group', 'replica'))
- grad_norm1: float32 [896], P('group')
- grad_qkv: float32 [896, 1152], P('group')
- grad_bias: float32 [1152], P('group')
- grad_out: float32 [896, 896], P('group')
- grad_norm2: float32 [896], P('group')
- grad_gate: float32 [896, 4864], P(None, 'group')
- grad_up: float32 [896, 4864], P(None, 'group')
- grad_down: float32 [4864, 896], P('group')
Inputs may be any that keep to these rules, and one draw needn't show every extreme that they name: `segments`: segment ids never fall along a sequence.
All inputs are finite; a program needn't handle non-finite values.
Results may differ from a plain program's by a relative error of at most 0.023.
Values may be sent and summed in bfloat16 or wider, within the bound.
A program may use at most 192 MiB of HBM per device.

v0:
```python
import jax
import jax.numpy as jnp
from jax import lax
from jax.sharding import PartitionSpec as P

H = 14
KV = 2
HD = 64


EPSILON = 1e-06
ROPE_BASE = 1000000.0
NEG_LARGE = -1e30


def doc_layout(segments, head_dim):
    length = segments.shape[1]
    places = jnp.arange(length, dtype=jnp.int32)
    same_doc = segments[:, :, None] == segments[:, None, :]
    earlier = places[None, None, :] < places[None, :, None]
    positions = jnp.sum(jnp.where(same_doc & earlier, 1.0, 0.0).astype(jnp.float32), axis=2)
    allowed = jnp.where(same_doc & (places[None, None, :] <= places[None, :, None]), 1, 0).astype(
        jnp.int32
    )
    half_dim = head_dim // 2
    frequency = ROPE_BASE ** (-2.0 * jnp.arange(half_dim, dtype=jnp.float32) / head_dim)
    angles = positions[:, :, None] * frequency[None, None, :]
    return (allowed, jnp.cos(angles)[:, :, None, :], jnp.sin(angles)[:, :, None, :])


def rotate(values, cosine, sine):
    half_dim = values.shape[-1] // 2
    front_half = values[..., :half_dim]
    back_half = values[..., half_dim:]
    return jnp.concatenate(
        [front_half * cosine - back_half * sine, back_half * cosine + front_half * sine], axis=-1
    )


def unrotate(gradients, cosine, sine):
    half_dim = gradients.shape[-1] // 2
    front_half = gradients[..., :half_dim]
    back_half = gradients[..., half_dim:]
    return jnp.concatenate(
        [front_half * cosine + back_half * sine, back_half * cosine - front_half * sine], axis=-1
    )


def inverse_rms(hidden):
    return lax.rsqrt(jnp.mean(hidden * hidden, axis=-1, keepdims=True) + EPSILON)


def norm_backward(hidden, inv_rms, gain_f, back_normed):
    weighted = back_normed * gain_f
    inner = jnp.mean(weighted * hidden, axis=-1, keepdims=True)
    back_hidden = inv_rms * weighted - hidden * (inv_rms * inv_rms * inv_rms) * inner
    back_gain = jnp.sum(back_normed * hidden * inv_rms, axis=0)
    return (back_hidden, back_gain)


def matmul(left, right):
    return jnp.dot(left, right, preferred_element_type=jnp.float32)


def outer_sum(left, right):
    return lax.dot_general(
        left, right, (((0,), (0,)), ((), ())), preferred_element_type=jnp.float32
    )


def times_transposed(left, right):
    return lax.dot_general(
        left, right, (((1,), (1,)), ((), ())), preferred_element_type=jnp.float32
    )


def score_block(query_b, keys_b, allowed, score_scale):
    scores = (
        jnp.einsum("sqkgd,spkd->skgqp", query_b, keys_b, preferred_element_type=jnp.float32)
        * score_scale
    )
    return jnp.where(allowed[:, None, None, :, :] > 0, scores, NEG_LARGE)


def on_device(
    tokens,
    segments,
    norm1_gain,
    qkv_weight,
    qkv_bias,
    out_weight,
    norm2_gain,
    gate_weight,
    up_weight,
    down_weight,
    cotangent,
):
    sequences, length, model_width = tokens.shape
    row_count = sequences * length
    q_width = H * HD
    kv_width = KV * HD
    groups = H // KV
    score_scale = HD ** (-0.5)
    gain1_b, w_qkv, b_qkv, w_out, gain2_b = (
        lax.all_gather(norm1_gain, "group", axis=0, tiled=True),
        lax.all_gather(qkv_weight, "group", axis=0, tiled=True),
        lax.all_gather(qkv_bias, "group", axis=0, tiled=True),
        lax.all_gather(out_weight, "group", axis=0, tiled=True),
        lax.all_gather(norm2_gain, "group", axis=0, tiled=True),
    )
    allowed, cosine, sine = doc_layout(segments, HD)
    resid_in = tokens.reshape(row_count, model_width).astype(jnp.float32)
    inv_rms1 = inverse_rms(resid_in)
    gain1 = gain1_b.astype(jnp.float32)
    normed1 = (resid_in * inv_rms1 * gain1).astype(jnp.bfloat16)
    projected = matmul(normed1, w_qkv) + b_qkv.astype(jnp.float32)
    query = projected[:, :q_width].reshape(sequences, length, H, HD)
    keys_raw = projected[:, q_width : q_width + kv_width].reshape(sequences, length, KV, HD)
    values_raw = projected[:, q_width + kv_width :].reshape(sequences, length, KV, HD)
    query_b = (
        rotate(query, cosine, sine).astype(jnp.bfloat16).reshape(sequences, length, KV, groups, HD)
    )
    keys_b = rotate(keys_raw, cosine, sine).astype(jnp.bfloat16)
    values_b = values_raw.astype(jnp.bfloat16)
    scores = score_block(query_b, keys_b, allowed, score_scale)
    top_score = jnp.max(scores, axis=-1, keepdims=True)
    log_total = top_score + jnp.log(jnp.sum(jnp.exp(scores - top_score), axis=-1, keepdims=True))
    soft_b = jnp.exp(scores - log_total).astype(jnp.bfloat16)
    context = jnp.einsum("skgqp,spkd->sqkgd", soft_b, values_b, preferred_element_type=jnp.float32)
    context_b = context.astype(jnp.bfloat16).reshape(row_count, q_width)
    middle = resid_in + matmul(context_b, w_out)
    inv_rms2 = inverse_rms(middle)
    gain2 = gain2_b.astype(jnp.float32)
    normed2 = (middle * inv_rms2 * gain2).astype(jnp.bfloat16)
    back_rows = cotangent.reshape(row_count, model_width)
    normed_all, back_all = (
        lax.all_gather(normed2, "group", axis=0, tiled=True),
        lax.all_gather(back_rows, "group", axis=0, tiled=True),
    )
    gate_pre = matmul(normed_all, gate_weight)
    up_proj = matmul(normed_all, up_weight)
    sigmoid_gate = jax.nn.sigmoid(gate_pre)
    silu_gate = gate_pre * sigmoid_gate
    activ_b = (silu_gate * up_proj).astype(jnp.bfloat16)
    result = middle + lax.psum_scatter(
        matmul(activ_b, down_weight).astype(jnp.bfloat16), "group", scatter_dimension=0, tiled=True
    ).astype(jnp.float32)
    back_activ = times_transposed(back_all, down_weight)
    back_gate = (
        back_activ * up_proj * sigmoid_gate * (1.0 + gate_pre * (1.0 - sigmoid_gate))
    ).astype(jnp.bfloat16)
    back_up = (back_activ * silu_gate).astype(jnp.bfloat16)
    grad_down = outer_sum(activ_b, back_all)
    grad_gate = outer_sum(normed_all, back_gate)
    grad_up = outer_sum(normed_all, back_up)
    local_normed = times_transposed(back_gate, gate_weight) + times_transposed(back_up, up_weight)
    back_normed2 = lax.psum_scatter(
        local_normed.astype(jnp.bfloat16), "group", scatter_dimension=0, tiled=True
    ).astype(jnp.float32)
    gain1_b, w_qkv, b_qkv, w_out, gain2_b = (
        lax.all_gather(norm1_gain, "group", axis=0, tiled=True),
        lax.all_gather(qkv_weight, "group", axis=0, tiled=True),
        lax.all_gather(qkv_bias, "group", axis=0, tiled=True),
        lax.all_gather(out_weight, "group", axis=0, tiled=True),
        lax.all_gather(norm2_gain, "group", axis=0, tiled=True),
    )
    gain1 = gain1_b.astype(jnp.float32)
    gain2 = gain2_b.astype(jnp.float32)
    back_norm2, grad_norm2_part = norm_backward(middle, inv_rms2, gain2, back_normed2)
    back_middle = back_rows.astype(jnp.float32) + back_norm2
    back_middle_b = back_middle.astype(jnp.bfloat16)
    grad_out_part = outer_sum(context_b, back_middle_b)
    back_context = times_transposed(back_middle_b, w_out).astype(jnp.bfloat16)
    back_context = back_context.reshape(sequences, length, KV, groups, HD)
    soft = jnp.exp(score_block(query_b, keys_b, allowed, score_scale) - log_total)
    soft_again = soft.astype(jnp.bfloat16)
    back_values = jnp.einsum(
        "skgqp,sqkgd->spkd", soft_again, back_context, preferred_element_type=jnp.float32
    )
    back_soft = jnp.einsum(
        "sqkgd,spkd->skgqp", back_context, values_b, preferred_element_type=jnp.float32
    )
    row_dot = jnp.sum(soft * back_soft, axis=-1, keepdims=True)
    back_scores = (soft * (back_soft - row_dot) * score_scale).astype(jnp.bfloat16)
    back_query = jnp.einsum(
        "skgqp,spkd->sqkgd", back_scores, keys_b, preferred_element_type=jnp.float32
    )
    back_keys = jnp.einsum(
        "skgqp,sqkgd->spkd", back_scores, query_b, preferred_element_type=jnp.float32
    )
    back_query = unrotate(back_query.reshape(sequences, length, H, HD), cosine, sine)
    back_keys = unrotate(back_keys, cosine, sine)
    back_proj = jnp.concatenate(
        [
            back_query.reshape(row_count, q_width),
            back_keys.reshape(row_count, kv_width),
            back_values.reshape(row_count, kv_width),
        ],
        axis=1,
    )
    grad_bias_part = jnp.sum(back_proj, axis=0)
    back_proj_b = back_proj.astype(jnp.bfloat16)
    grad_qkv_part = outer_sum(normed1, back_proj_b)
    back_normed1 = times_transposed(back_proj_b, w_qkv)
    back_norm1, grad_norm1_part = norm_backward(resid_in, inv_rms1, gain1, back_normed1)
    back_tokens = back_middle + back_norm1
    grad_norm1, grad_qkv, grad_bias, grad_out, grad_norm2 = (
        lax.psum_scatter(
            grad_norm1_part.astype(jnp.bfloat16), "group", scatter_dimension=0, tiled=True
        ).astype(jnp.float32),
        lax.psum_scatter(
            grad_qkv_part.astype(jnp.bfloat16), "group", scatter_dimension=0, tiled=True
        ).astype(jnp.float32),
        lax.psum_scatter(
            grad_bias_part.astype(jnp.bfloat16), "group", scatter_dimension=0, tiled=True
        ).astype(jnp.float32),
        lax.psum_scatter(
            grad_out_part.astype(jnp.bfloat16), "group", scatter_dimension=0, tiled=True
        ).astype(jnp.float32),
        lax.psum_scatter(
            grad_norm2_part.astype(jnp.bfloat16), "group", scatter_dimension=0, tiled=True
        ).astype(jnp.float32),
    )
    grad_norm1, grad_qkv, grad_bias, grad_out, grad_norm2, grad_gate, grad_up, grad_down = (
        lax.psum(grad_norm1.astype(jnp.bfloat16), "replica").astype(jnp.float32),
        lax.psum(grad_qkv.astype(jnp.bfloat16), "replica").astype(jnp.float32),
        lax.psum(grad_bias.astype(jnp.bfloat16), "replica").astype(jnp.float32),
        lax.psum(grad_out.astype(jnp.bfloat16), "replica").astype(jnp.float32),
        lax.psum(grad_norm2.astype(jnp.bfloat16), "replica").astype(jnp.float32),
        lax.psum(grad_gate.astype(jnp.bfloat16), "replica").astype(jnp.float32),
        lax.psum(grad_up.astype(jnp.bfloat16), "replica").astype(jnp.float32),
        lax.psum(grad_down.astype(jnp.bfloat16), "replica").astype(jnp.float32),
    )
    shape_out = (sequences, length, model_width)
    return (
        result.reshape(shape_out),
        back_tokens.reshape(shape_out),
        grad_norm1,
        grad_qkv,
        grad_bias,
        grad_out,
        grad_norm2,
        grad_gate,
        grad_up,
        grad_down,
    )


def solution(mesh):
    in_specs = (
        P(("group", "replica"), None, None),
        P(("group", "replica"), None),
        P("group"),
        P("group", None),
        P("group"),
        P("group", None),
        P("group"),
        P(None, "group"),
        P(None, "group"),
        P("group", None),
        P(("group", "replica"), None, None),
    )
    out_specs = (
        P(("group", "replica"), None, None),
        P(("group", "replica"), None, None),
        P("group"),
        P("group", None),
        P("group"),
        P("group", None),
        P("group"),
        P(None, "group"),
        P(None, "group"),
        P("group", None),
    )
    return jax.shard_map(
        on_device, mesh=mesh, in_specs=in_specs, out_specs=out_specs, check_vma=False
    )
```

profile of v0, /device:TPU:0, one launch (start us, length us, event | category | flops | bytes accessed | tf_op | source)
XLA Modules:
  0.0 505.1 jit_solution(13327327023692084482)
XLA Ops:
  7.3 0.7 all-gather.4.cloned.1.call-update
  8.0 0.7 all-gather.6.cloned.1.call-update
  8.8 0.9 select_reduce_fusion
  9.7 0.9 select_compare_fusion
  10.6 1.3 fusion.50
  13.4 0.6 multiply_multiply_fusion
  14.7 5.9 %all-reduce.9 = (bf16[1152]{0:T(1024)(128)(2,1)S(1)}, bf16[896]{0:T(1024)(128)(2,1)S(1)}, bf16[896]{0:T(1024)(128)(2,1)S(1)}) all-reduce(bf16[1152]{0:T(1024)(128)(2,1)S(1)} %dynamic-update-slice.1, bf16[896]{0:T(1024)(128)(2,1)S(1)} %dynamic-update-slice, ...), channel_id=1, replica_groups=mesh['group'=2,'replica'=16] {'group'}, use_global_device_ids=true, to_apply=%add.1 | all-reduce | flops 2944 | bytes 11776
  21.0 14.6 %all-gather = bf16[1,288,896]{2,1,0:T(8,128)(2,1)} all-gather(bf16[1,144,896]{2,1,0:T(8,128)(2,1)S(1)} %copy-done.6), channel_id=2, replica_groups=mesh['group'=2,'replica'=16] {'group'}, dimensions={1}, use_global_device_ids=true | all-gather | bytes 774144 | tf_op jit(solution)/shard_map/all_gather | solution.py:138
  35.6 15.0 %all-gather.4.cloned.1.call-done = bf16[896,1152]{1,0:T(8,128)(2,1)} async-done(((bf16[448,1152]{1,0:T(8,128)(2,1)}), bf16[896,1152]{1,0:T(8,128)(2,1)}) %all-gather.4.cloned.1.call-update) | async-done | bytes 2064400 | tf_op jit(solution)/shard_map/all_gather | solution.py:106
  50.6 2.2 convolution_add_fusion
  53.2 0.3 reshape.421
  53.5 0.6 subtract_convert_fusion
  54.1 0.5 copy.79
  54.6 0.5 copy.80
  55.1 0.5 fusion.51
  55.7 0.3 exponential_reduce_fusion
  56.0 0.5 convolution_convert_fusion.6
  56.6 23.2 %all-gather.6.cloned.1.call-done = bf16[896,896]{1,0:T(8,128)(2,1)} async-done(((bf16[448,896]{1,0:T(8,128)(2,1)}), bf16[896,896]{1,0:T(8,128)(2,1)}) %all-gather.6.cloned.1.call-update) | async-done | bytes 1605648 | tf_op jit(solution)/shard_map/all_gather | solution.py:108
  79.8 2.0 multiply_reduce_fusion
  82.0 8.9 %all_gather.30 = bf16[288,896]{1,0:T(8,128)(2,1)S(1)} all-gather(bf16[144,896]{1,0:T(8,128)(2,1)S(1)} %multiply_convert_fusion.3), channel_id=1, replica_groups=mesh['group'=2,'replica'=16] {'group'}, dimensions={0}, use_global_device_ids=true | all-gather | bytes 774144 | tf_op jit(solution)/shard_map/all_gather | solution.py:137
  91.0 4.1 fusion.53
  95.2 1.7 fusion.52
  96.9 4.0 multiply_convert_fusion
  100.9 1.7 fusion.54
  102.7 2.5 fusion.6
  105.3 5.1 %convolution_convert_fusion.5 = bf16[288,896]{1,0:T(8,128)(2,1)} fusion(bf16[288,2432]{1,0:T(8,128)(2,1)} %get-tuple-element.30, bf16[2432,896]{1,0:T(8,128)(2,1)} %param.20), kind=kOutput, calls=%fused_computation.22 | convolution fusion | flops 1255403520 | bytes 6275072 | tf_op jit(solution)/shard_map/dot_general | solution.py:62
  110.5 9.4 %reduce-scatter.7.cloned.1.call-done = bf16[144,896]{1,0:T(8,128)(2,1)} async-done(((bf16[288,896]{1,0:T(8,128)(2,1)}), bf16[144,896]{1,0:T(8,128)(2,1)}) %reduce-scatter.7.cloned.1.call-update) | async-done | bytes 258064 | tf_op jit(solution)/shard_map/reduce_scatter | solution.py:157
  119.8 1.1 fusion.15
  121.0 16.1 %reduce-scatter.5.cloned.1.call-done = bf16[144,896]{1,0:T(8,128)(2,1)} async-done(((bf16[288,896]{1,0:T(8,128)(2,1)}), bf16[144,896]{1,0:T(8,128)(2,1)}) %reduce-scatter.5.cloned.1.call-update) | async-done | bytes 258064 | tf_op jit(solution)/shard_map/reduce_scatter | solution.py:145
  137.1 2.2 fusion.12
  139.3 3.0 convolution_convert_fusion.4
  142.3 0.3 reduce-scatter.9.cloned.1.call-start
  142.6 2.7 convolution_convert_fusion.7
  145.3 1.1 copy.107
  146.5 0.5 fusion.31
  147.1 0.6 fusion.1
  147.7 0.6 fusion.8
  148.3 0.4 copy-done.8
  148.9 0.5 convolution_bitcast_fusion
  149.7 0.3 fusion.40
  150.1 0.6 copy.109
  150.7 0.6 copy.108
  151.3 0.3 multiply_add_fusion
  151.6 0.4 pad_maximum_fusion
  152.0 0.3 reshape.429
  152.3 2.2 convolution_convert_fusion.3
  154.6 0.3 all-reduce.12.cloned.1.call-start
  154.9 4.7 convolution_convert_fusion
  159.6 4.6 convolution_convert_fusion.1
  164.2 4.6 convolution_convert_fusion.2
  168.9 34.2 %reduce-scatter.9.cloned.1.call-done = bf16[448,1152]{1,0:T(8,128)(2,1)} async-done(((bf16[896,1152]{1,0:T(8,128)(2,1)}), bf16[448,1152]{1,0:T(8,128)(2,1)}) %reduce-scatter.9.cloned.1.call-update) | async-done | bytes 1032208 | tf_op jit(solution)/shard_map/reduce_scatter | solution.py:211
  204.7 1.6 fusion.25
  206.3 5.0 all-reduce.8
  211.5 33.8 %all-reduce.6 = (bf16[448]{0:T(512)(128)(2,1)S(1)}, bf16[576]{0:T(1024)(128)(2,1)S(1)}, bf16[448]{0:T(512)(128)(2,1)S(1)}) all-reduce(bf16[448]{0:T(512)(128)(2,1)S(1)} %dynamic-slice.4, bf16[576]{0:T(1024)(128)(2,1)S(1)} %dynamic-slice.6, bf16[448]{0:T(512)(128)(2,1)S(1)} %dynamic-slice.8), channel_id=1, replica_groups=mesh['group'=2,'replica'=16] {'replica'}, use_global_device_ids=true, to_apply=%region_12.13 | all-reduce | flops 1472 | bytes 5888 | tf_op jit(solution)/shard_map/psum | solution.py:225
  245.2 0.6 convert_element_type.174
  245.8 0.6 convert_element_type.182
  246.4 0.6 convert_element_type.178
  247.0 2.1 fusion.22
  249.1 232.0 %all-reduce.12.cloned.1.call-done = (bf16[448,1152]{1,0:T(8,128)(2,1)}, bf16[448,896]{1,0:T(8,128)(2,1)}, bf16[896,2432]{1,0:T(8,128)(2,1)}, bf16[896,2432]{1,0:T(8,128)(2,1)}, bf16[2432,896]{1,0:T(8,128)(2,1)}) async-done(((bf16[448,1152]{1,0:T(8,128)(2,1)}, bf16[448,896]{1,0:T(8,128)(2,1)}, bf16[896,2432]{1,0:T(8,128)(2,1)}, bf16[896,2432]{1,0:T(8,128)(2,1)}, bf16[2432,896]{1,0:T(8,128)(2,1)}), ...) | async-done | bytes 14909456 | tf_op jit(solution)/shard_map/psum | solution.py:226
  481.1 2.8 convert_element_type.176
  483.9 1.3 convert_element_type.180
  485.2 4.9 convert_element_type.184
  490.1 4.1 convert_element_type.186
  494.1 4.1 convert_element_type.188
  (140 shorter events, 3.3 us)
Async XLA Ops:
  7.2 6.1 %copy-start.2 = (bf16[1,144,896]{2,1,0:T(8,128)(2,1)S(1)}, bf16[1,144,896]{2,1,0:T(8,128)(2,1)}, u32[]{:S(2)}) copy-start(bf16[1,144,896]{2,1,0:T(8,128)(2,1)} %param.11) | copy-start | bytes 774148
  7.2 6.8 %copy-start.28 = (bf16[448]{0:T(512)(128)(2,1)S(1)}, bf16[448]{0:T(512)(128)(2,1)}, u32[]{:S(2)}) copy-start(bf16[448]{0:T(512)(128)(2,1)} %param.13) | copy-start | bytes 2692
  7.2 7.0 %copy-start.29 = (bf16[448]{0:T(512)(128)(2,1)S(1)}, bf16[448]{0:T(512)(128)(2,1)}, u32[]{:S(2)}) copy-start(bf16[448]{0:T(512)(128)(2,1)} %param.17) | copy-start | bytes 2692
  7.2 7.2 %copy-start.27 = (bf16[576]{0:T(1024)(128)(2,1)S(1)}, bf16[576]{0:T(1024)(128)(2,1)}, u32[]{:S(2)}) copy-start(bf16[576]{0:T(1024)(128)(2,1)} %param.15) | copy-start | bytes 3460
  7.2 13.8 %copy-start.6 = (bf16[1,144,896]{2,1,0:T(8,128)(2,1)S(1)}, bf16[1,144,896]{2,1,0:T(8,128)(2,1)}, u32[]{:S(2)}) copy-start(bf16[1,144,896]{2,1,0:T(8,128)(2,1)} %param.21) | copy-start | bytes 774148
  7.2 43.4 %all-gather.4.cloned.1.call-start = ((), (), s32[]{:S(2)}) async-start(), calls=%async_computation.4 | async-start | bytes 3096576 | tf_op jit(solution)/shard_map/all_gather | solution.py:106
  8.0 71.8 %all-gather.6.cloned.1.call-start = ((), (), s32[]{:S(2)}) async-start(), calls=%async_computation.5 | async-start | bytes 2408448 | tf_op jit(solution)/shard_map/all_gather | solution.py:108
  8.7 111.1 %reduce-scatter.7.cloned.1.call-start = ((), (), s32[]{:S(2)}) async-start(), calls=%async_computation.7 | async-start | bytes 774144 | tf_op jit(solution)/shard_map/reduce_scatter | solution.py:157
  20.8 34.3 %copy-start.16 = (f32[144,32]{0,1:T(8,128)}, f32[144,32]{0,1:T(8,128)S(1)}, u32[]{:S(2)}) copy-start(f32[144,32]{0,1:T(8,128)S(1)} %get-tuple-element.44) | copy-start | bytes 55300
  20.9 32.6 %copy-start.12 = (f32[144,32]{1,0:T(8,128)}, f32[144,32]{1,0:T(8,128)S(1)}, u32[]{:S(2)}) copy-start(f32[144,32]{1,0:T(8,128)S(1)} %copy.77) | copy-start | bytes 55300
  21.0 32.5 %copy-start.14 = (f32[144,32]{1,0:T(8,128)}, f32[144,32]{1,0:T(8,128)S(1)}, u32[]{:S(2)}) copy-start(f32[144,32]{1,0:T(8,128)S(1)} %copy.78) | copy-start | bytes 55300
  54.6 1.4 copy-start.7
  55.1 0.9 copy-start.9
  55.1 0.9 copy-start.22
  55.1 0.9 copy-start.24
  56.5 34.4 %copy-start.4 = (bf16[2,64,7,144]{3,1,2,0:T(8,128)(2,1)}, bf16[2,64,7,144]{3,1,2,0:T(8,128)(2,1)S(1)}, u32[]{:S(2)}) copy-start(bf16[2,64,7,144]{3,1,2,0:T(8,128)(2,1)S(1)} %convolution_convert_fusion.6) | copy-start | bytes 774148
  82.0 13.1 %slice-start.4 = ((s8[4358144]{0:T(1024)(128)(4,1)}), s8[4194304]{0:T(1024)(128)(4,1)S(1)}, s32[]{:S(2)}) async-start(s8[4358144]{0:T(1024)(128)(4,1)} %bitcast.142), calls=%async_computation.15 | async-start | bytes 8388608
  90.9 4.2 copy-start.20
  90.9 4.2 slice-start.5
  91.0 5.9 %slice-start.8 = ((s8[4358144]{0:T(1024)(128)(4,1)}), s8[4194304]{0:T(1024)(128)(4,1)S(1)}, s32[]{:S(2)}) async-start(s8[4358144]{0:T(1024)(128)(4,1)} %bitcast.146), calls=%async_computation.19 | async-start | bytes 8388608
  95.2 1.7 copy-start.18
  95.2 1.7 slice-start.9
  95.2 7.5 %slice-start.6 = ((s8[4358144]{0:T(1024)(128)(4,1)}), s8[4194304]{0:T(1024)(128)(4,1)S(1)}, s32[]{:S(2)}) async-start(s8[4358144]{0:T(1024)(128)(4,1)} %bitcast.144), calls=%async_computation.17 | async-start | bytes 8388608
  96.9 5.8 %slice-start.7 = ((s8[4358144]{0:T(1024)(128)(4,1)}), s8[163840]{0:T(1024)(128)(4,1)S(1)}, s32[]{:S(2)}) async-start(s8[4358144]{0:T(1024)(128)(4,1)} %bitcast.144), calls=%async_computation.18 | async-start | bytes 327680
  100.9 1.7 copy-start.31
  100.9 1.7 copy-start.33
  105.2 31.9 %reduce-scatter.5.cloned.1.call-start = ((), (), s32[]{:S(2)}) async-start(), calls=%async_computation.6 | async-start | bytes 774144 | tf_op jit(solution)/shard_map/reduce_scatter | solution.py:145
  110.4 58.5 %reduce-scatter.11.cloned.1.call-start = ((), (), s32[]{:S(2)}) async-start(), calls=%async_computation.9 | async-start | bytes 2408448 | tf_op jit(solution)/shard_map/reduce_scatter | solution.py:217
  139.3 3.3 copy-start
  142.3 60.8 %reduce-scatter.9.cloned.1.call-start = ((), (), s32[]{:S(2)}) async-start(), calls=%async_computation.8 | async-start | bytes 3096576 | tf_op jit(solution)/shard_map/reduce_scatter | solution.py:211
  147.7 1.0 copy-start.8
  147.7 1.2 copy-start.10
  147.7 1.7 copy-start.17
  148.9 0.8 copy-start.23
  148.9 0.8 copy-start.25
  150.1 1.2 copy-start.13
  150.1 1.2 copy-start.15
  152.3 2.6 copy-start.19
  152.3 2.6 copy-start.30
  154.6 5.1 %copy-start.21 = (bf16[288,896]{1,0:T(8,128)(2,1)S(1)}, bf16[288,896]{1,0:T(8,128)(2,1)}, u32[]{:S(2)}) copy-start(bf16[288,896]{1,0:T(8,128)(2,1)} %copy-done.20) | copy-start | bytes 1548292
  154.6 326.5 %all-reduce.12.cloned.1.call-start = ((), (), s32[]{:S(2)}) async-start(), calls=%async_computation.10 | async-start | bytes 29818880 | tf_op jit(solution)/shard_map/psum | solution.py:226
  154.9 4.7 copy-start.34
  159.6 4.6 copy-start.32
  203.1 1.6 copy-start.5
  204.6 42.4 %copy-start.1 = (f32[144,896]{1,0:T(8,128)S(1)}, f32[144,896]{1,0:T(8,128)}, u32[]{:S(2)}) copy-start(f32[144,896]{1,0:T(8,128)} %copy-done) | copy-start | bytes 1548292
  204.6 42.4 %copy-start.26 = (f32[144]{0:T(256)S(1)}, f32[144]{0:T(256)}, u32[]{:S(2)}) copy-start(f32[144]{0:T(256)} %get-tuple-element.45) | copy-start | bytes 1732
  481.1 2.8 copy-start.11
  481.1 4.1 copy-start.3
  483.9 6.1 %slice-start.2 = ((s8[4358144]{0:T(1024)(128)(4,1)}), s8[4194304]{0:T(1024)(128)(4,1)S(1)}, s32[]{:S(2)}) async-start(s8[4358144]{0:T(1024)(128)(4,1)} %bitcast.125), calls=%async_computation.13 | async-start | bytes 8388608
  485.2 4.9 slice-start.3
  485.2 9.0 %slice-start = ((s8[4358144]{0:T(1024)(128)(4,1)}), s8[4194304]{0:T(1024)(128)(4,1)S(1)}, s32[]{:S(2)}) async-start(s8[4358144]{0:T(1024)(128)(4,1)} %bitcast.123), calls=%async_computation.11 | async-start | bytes 8388608
  490.1 4.1 slice-start.1
Sparse Core Ops, SparseCore 0:
  9.6 40.9 all-gather.3
  52.2 27.5 all-gather.5
  105.3 14.4 reduce-scatter.6
  122.6 14.4 reduce-scatter.4
  142.4 26.4 reduce-scatter.10
  171.6 31.4 reduce-scatter.8
  209.3 271.7 all-reduce.11
where the time goes:
time: 506 us; the launch traced here: 505 us
  waiting for transfers between devices  332 us (66%)
  blocking collectives  68.2 us (13%)
  matrix products  49.6 us (10%)
  other arithmetic  29.5 us (6%)
  between operations  17.6 us (3%)
  local copies, waits for them, and re-layouts  7.93 us (2%)
    psum x1, waiting for transfers between devices, on_device(): lax.psum(grad_qkv.astype(jnp.bfloat16), 'replica').astype(jnp.float32)  232 us
    reduce_scatter x1, waiting for transfers between devices, on_device(): lax.psum_scatter(grad_qkv_part.astype(jnp.bfloat16), 'group', scatter_dim...  34.2 us
    psum x1, blocking collectives, on_device(): lax.psum(grad_norm1.astype(jnp.bfloat16), 'replica').astype(jnp.float32)  33.8 us
    all_gather x1, waiting for transfers between devices, on_device(): lax.all_gather(out_weight, 'group', axis=0, tiled=True)  23.2 us
    dot_general x5, matrix products, outer_sum(): lax.dot_general(left, right, (((0,), (0,)), ((), ())), preferred_element_...  19.1 us
    reduce_scatter x1, waiting for transfers between devices, on_device(): lax.psum_scatter(matmul(activ_b, down_weight).astype(jnp.bfloat16), 'grou...  16.1 us
    dot_general x5, matrix products, matmul(): return jnp.dot(left, right, preferred_element_type=jnp.float32)  15.2 us
    all_gather x1, waiting for transfers between devices, on_device(): lax.all_gather(qkv_weight, 'group', axis=0, tiled=True)  15 us
  transfers between devices with their start and end apart: 7, of which 7 were waited for; matrix products, arithmetic and copies ran while one was open for 9% of the time, Pallas kernels for 0%

commit v1 on v0

--- a/solution.py
+++ b/solution.py
@@ -1,6 +1,10 @@
+import functools
+
 import jax
 import jax.numpy as jnp
 from jax import lax
+from jax.experimental import pallas as pl
+from jax.experimental.pallas import tpu as pltpu
 from jax.sharding import PartitionSpec as P
 
 H = 14
@@ -80,6 +84,249 @@
         * score_scale
     )
     return jnp.where(allowed[:, None, None, :, :] > 0, scores, NEG_LARGE)
+
+
+def stage_bits(copies, far_first):
+    bits = [1 << i for i in range(copies.bit_length() - 1)]
+    if far_first:
+        bits = bits[:1] + bits[2:] + bits[1:2]
+    return bits
+
+
+def sum_kernel(copies, pieces, count, *refs):
+    ins, outs = refs[:count], refs[count : 2 * count]
+    n = len(pieces)
+    held = refs[2 * count : 2 * count + n]
+    landed = refs[2 * count + n : 2 * count + 2 * n]
+    final = refs[2 * count + 2 * n : 2 * count + 3 * n]
+    send_sem, recv_sem, local_sem = refs[2 * count + 3 * n :]
+    me = lax.axis_index("replica")
+    stages = copies.bit_length() - 1
+
+    def partner(bit):
+        return me + bit * (1 - 2 * (lax.div(me, bit) % 2))
+
+    loads = []
+    for p, (which, start, width, _) in enumerate(pieces):
+        load = pltpu.make_async_copy(
+            ins[which].at[:, :, pl.ds(start, width)], held[p], local_sem.at[p, 0]
+        )
+        load.start()
+        loads.append(load)
+    barrier = pltpu.get_barrier_semaphore()
+    for i in range(stages):
+        pl.semaphore_signal(
+            barrier,
+            inc=1,
+            device_id={"replica": partner(1 << i)},
+            device_id_type=pl.DeviceIdType.MESH,
+        )
+    pl.semaphore_wait(barrier, stages)
+
+    bits = [stage_bits(copies, far) for (_, _, _, far) in pieces]
+    base = [0] * n
+    trail = [[] for _ in range(n)]
+    copying = [None] * n
+    for k in range(stages + 1):
+        size = copies >> (k + 1)
+        offset = copies - (copies >> k)
+        for p in range(n):
+            if k == 0:
+                loads[p].wait()
+            else:
+                copying[p].wait()
+                old, previous = copies >> k, copies - (copies >> (k - 1))
+                first = base[p]
+
+                goal = held[p] if k < stages else final[p]
+
+                def add(i, carry, p=p, goal=goal, first=first, previous=previous):
+                    goal[first + i] = held[p][first + i] + landed[p][previous + i]
+                    return carry
+
+                lax.fori_loop(0, old, add, 0)
+            if k < stages:
+                bit = bits[p][k]
+                side = lax.div(me, bit) % 2
+                keep, give = base[p] + side * size, base[p] + (1 - side) * size
+                copy = pltpu.make_async_remote_copy(
+                    src_ref=held[p].at[pl.ds(give, size)],
+                    dst_ref=landed[p].at[pl.ds(offset, size)],
+                    send_sem=send_sem.at[p, k],
+                    recv_sem=recv_sem.at[p, k],
+                    device_id={"replica": partner(bit)},
+                    device_id_type=pl.DeviceIdType.MESH,
+                )
+                trail[p].append(keep)
+                base[p] = keep
+            else:
+                copy = spread(final, send_sem, recv_sem, trail, bits, partner, p, k - 1, copies)
+            copy.start()
+            copying[p] = copy
+    stores = []
+    for k in range(stages - 1, -1, -1):
+        for p, (which, start, width, _) in enumerate(pieces):
+            copying[p].wait()
+            if k > 0:
+                copying[p] = spread(
+                    final, send_sem, recv_sem, trail, bits, partner, p, k - 1, copies
+                )
+                copying[p].start()
+            else:
+                store = pltpu.make_async_copy(
+                    final[p], outs[which].at[:, :, pl.ds(start, width)], local_sem.at[p, 1]
+                )
+                store.start()
+                stores.append(store)
+    for store in stores:
+        store.wait()
+
+
+def spread(final, send_sem, recv_sem, trail, bits, partner, p, k, copies):
+    block = final[p].at[pl.ds(trail[p][k], copies >> (k + 1))]
+    stages = copies.bit_length() - 1
+    return pltpu.make_async_remote_copy(
+        src_ref=block,
+        dst_ref=block,
+        send_sem=send_sem.at[p, stages + k],
+        recv_sem=recv_sem.at[p, stages + k],
+        device_id={"replica": partner(bits[p][k])},
+        device_id_type=pl.DeviceIdType.MESH,
+    )
+
+
+def replica_sum(arrays, copies):
+    pieces = []
+    for which, array in enumerate(arrays):
+        columns = array.shape[2]
+        cut = -(-columns // 256) * 128
+        if columns > 1024:
+            pieces += [(which, 0, cut, False), (which, cut, columns - cut, True)]
+        else:
+            half = columns // 256 * 128
+            pieces += [(which, 0, half, True), (which, half, columns - half, False)]
+    stages = copies.bit_length() - 1
+    n, count = len(pieces), len(arrays)
+    shapes = [(arrays[w].shape[1], width) for (w, _, width, _) in pieces]
+    any_spec = pl.BlockSpec(memory_space=pltpu.HBM)
+    return pl.pallas_call(
+        functools.partial(sum_kernel, copies, tuple(pieces), count),
+        out_shape=[jax.ShapeDtypeStruct(a.shape, a.dtype) for a in arrays],
+        in_specs=[any_spec] * count,
+        out_specs=[any_spec] * count,
+        scratch_shapes=[pltpu.VMEM((copies, r, c), jnp.bfloat16) for r, c in shapes]
+        + [pltpu.VMEM((copies - 1, r, c), jnp.bfloat16) for r, c in shapes]
+        + [pltpu.VMEM((copies, r, c), jnp.bfloat16) for r, c in shapes]
+        + [
+            pltpu.SemaphoreType.DMA((n, 2 * stages)),
+            pltpu.SemaphoreType.DMA((n, 2 * stages)),
+            pltpu.SemaphoreType.DMA((n, 2)),
+        ],
+        compiler_params=pltpu.CompilerParams(
+            collective_id=0, has_side_effects=True, vmem_limit_bytes=52 * 1024 * 1024
+        ),
+        name="replica_sum",
+    )(*arrays)
+
+
+def swap(values):
+    return lax.ppermute(values, "group", [(0, 1), (1, 0)])
+
+
+def gather_weight(shard, pairs, copies):
+    if pairs != 2 or copies % 2:
+        return lax.all_gather(shard, "group", axis=0, tiled=True)
+    half = shard.shape[0] // 2
+    core = lax.axis_index("replica") % 2
+    mine = swap(lax.dynamic_slice_in_dim(shard, core * half, half, 0))
+    sibling = lax.ppermute(mine, "replica", [(i, i + 1 - 2 * (i % 2)) for i in range(copies)])
+    front = jnp.where(core == 0, mine, sibling)
+    back = jnp.where(core == 0, sibling, mine)
+    first = lax.axis_index("group") == 0
+    other = jnp.concatenate([front, back], axis=0)
+    return jnp.concatenate(
+        [jnp.where(first, shard, other), jnp.where(first, other, shard)], axis=0
+    )
+
+
+def gather_vectors(vectors, pairs):
+    if pairs != 2:
+        return [lax.all_gather(v, "group", axis=0, tiled=True) for v in vectors]
+    joined = jnp.concatenate(vectors)
+    other = swap(joined)
+    first = lax.axis_index("group") == 0
+    low, high = jnp.where(first, joined, other), jnp.where(first, other, joined)
+    found, at = [], 0
+    for v in vectors:
+        size = v.shape[0]
+        found.append(jnp.concatenate([low[at : at + size], high[at : at + size]]))
+        at += size
+    return found
+
+
+def gather_rows(rows, pairs):
+    if pairs != 2:
+        return lax.all_gather(rows, "group", axis=0, tiled=True)
+    return jnp.concatenate([rows, swap(rows)], axis=0)
+
+
+def scatter_rows(partial, pairs):
+    if pairs != 2:
+        return lax.psum_scatter(
+            partial.astype(jnp.bfloat16), "group", scatter_dimension=0, tiled=True
+        ).astype(jnp.float32)
+    half = partial.shape[0] // 2
+    return partial[:half] + swap(partial[half:].astype(jnp.bfloat16)).astype(jnp.float32)
+
+
+def scatter_owned(partial, pairs):
+    if pairs != 2:
+        return lax.psum_scatter(
+            partial.astype(jnp.bfloat16), "group", scatter_dimension=0, tiled=True
+        ).astype(jnp.float32)
+    half = partial.shape[0] // 2
+    me = lax.axis_index("group")
+    give = lax.dynamic_slice_in_dim(partial.astype(jnp.bfloat16), (1 - me) * half, half, 0)
+    keep = lax.dynamic_slice_in_dim(partial, me * half, half, 0)
+    return keep + swap(give).astype(jnp.float32)
+
+
+def sum_owned(small, qkv, out, gate, up, down, copies):
+    rows, width = qkv.shape[0], qkv.shape[1] + out.shape[1]
+    lines = 64
+    fits = (
+        copies == 16
+        and width % 256 == 0
+        and rows + 64 == copies // 2 * 64
+        and small.shape[0] <= width
+        and all(a.shape[0] % (8 * copies) == 0 and a.shape[1] % 128 == 0 for a in (gate, up, down))
+    )
+    if not fits:
+        return lax.psum(
+            tuple(a.astype(jnp.bfloat16) for a in (small, qkv, out, gate, up, down)), "replica"
+        )
+    joined = jnp.concatenate([qkv, out], axis=1)
+    line = jnp.pad(small, (0, width - small.shape[0]))[None, :]
+    joined = jnp.concatenate(
+        [joined, jnp.pad(line, ((0, lines - 1), (0, 0)))], axis=0
+    ).astype(jnp.bfloat16)
+    half = width // 2
+    joined = jnp.stack([joined[:, :half], joined[:, half:]]).reshape(copies, lines, half)
+    folded = [
+        a.astype(jnp.bfloat16).reshape(copies, a.shape[0] // copies, a.shape[1])
+        for a in (gate, up, down)
+    ]
+    gate_s, up_s, down_s, joined = replica_sum([*folded, joined], copies)
+    joined = joined.reshape(2, rows + lines, half)
+    joined = jnp.concatenate([joined[0], joined[1]], axis=1)
+    return (
+        joined[rows, : small.shape[0]],
+        joined[:rows, : qkv.shape[1]],
+        joined[:rows, qkv.shape[1] :],
+        gate_s.reshape(gate.shape),
+        up_s.reshape(up.shape),
+        down_s.reshape(down.shape),
+    )
 
 
 def on_device(
@@ -94,6 +341,9 @@
     up_weight,
     down_weight,
     cotangent,
+    *,
+    pairs,
+    copies,
 ):
     sequences, length, model_width = tokens.shape
     row_count = sequences * length
@@ -101,13 +351,10 @@
     kv_width = KV * HD
     groups = H // KV
     score_scale = HD ** (-0.5)
-    gain1_b, w_qkv, b_qkv, w_out, gain2_b = (
-        lax.all_gather(norm1_gain, "group", axis=0, tiled=True),
-        lax.all_gather(qkv_weight, "group", axis=0, tiled=True),
-        lax.all_gather(qkv_bias, "group", axis=0, tiled=True),
-        lax.all_gather(out_weight, "group", axis=0, tiled=True),
-        lax.all_gather(norm2_gain, "group", axis=0, tiled=True),
-    )
+    gain1_b, b_qkv, gain2_b = gather_vectors([norm1_gain, qkv_bias, norm2_gain], pairs)
+    w_qkv = gather_weight(qkv_weight, pairs, copies)
+    back_all = gather_rows(cotangent.reshape(row_count, model_width), pairs)
+    w_out = gather_weight(out_weight, pairs, copies)
     allowed, cosine, sine = doc_layout(segments, HD)
     resid_in = tokens.reshape(row_count, model_width).astype(jnp.float32)
     inv_rms1 = inverse_rms(resid_in)
@@ -133,18 +380,13 @@
     gain2 = gain2_b.astype(jnp.float32)
     normed2 = (middle * inv_rms2 * gain2).astype(jnp.bfloat16)
     back_rows = cotangent.reshape(row_count, model_width)
-    normed_all, back_all = (
-        lax.all_gather(normed2, "group", axis=0, tiled=True),
-        lax.all_gather(back_rows, "group", axis=0, tiled=True),
-    )
+    normed_all = gather_rows(normed2, pairs)
     gate_pre = matmul(normed_all, gate_weight)
     up_proj = matmul(normed_all, up_weight)
     sigmoid_gate = jax.nn.sigmoid(gate_pre)
     silu_gate = gate_pre * sigmoid_gate
     activ_b = (silu_gate * up_proj).astype(jnp.bfloat16)
-    result = middle + lax.psum_scatter(
-        matmul(activ_b, down_weight).astype(jnp.bfloat16), "group", scatter_dimension=0, tiled=True
-    ).astype(jnp.float32)
+    result = middle + scatter_rows(matmul(activ_b, down_weight), pairs)
     back_activ = times_transposed(back_all, down_weight)
     back_gate = (
         back_activ * up_proj * sigmoid_gate * (1.0 + gate_pre * (1.0 - sigmoid_gate))
@@ -154,18 +396,7 @@
     grad_gate = outer_sum(normed_all, back_gate)
     grad_up = outer_sum(normed_all, back_up)
     local_normed = times_transposed(back_gate, gate_weight) + times_transposed(back_up, up_weight)
-    back_normed2 = lax.psum_scatter(
-        local_normed.astype(jnp.bfloat16), "group", scatter_dimension=0, tiled=True
-    ).astype(jnp.float32)
-    gain1_b, w_qkv, b_qkv, w_out, gain2_b = (
-        lax.all_gather(norm1_gain, "group", axis=0, tiled=True),
-        lax.all_gather(qkv_weight, "group", axis=0, tiled=True),
-        lax.all_gather(qkv_bias, "group", axis=0, tiled=True),
-        lax.all_gather(out_weight, "group", axis=0, tiled=True),
-        lax.all_gather(norm2_gain, "group", axis=0, tiled=True),
-    )
-    gain1 = gain1_b.astype(jnp.float32)
-    gain2 = gain2_b.astype(jnp.float32)
+    back_normed2 = scatter_rows(local_normed, pairs)
     back_norm2, grad_norm2_part = norm_backward(middle, inv_rms2, gain2, back_normed2)
     back_middle = back_rows.astype(jnp.float32) + back_norm2
     back_middle_b = back_middle.astype(jnp.bfloat16)
@@ -204,32 +435,28 @@
     back_normed1 = times_transposed(back_proj_b, w_qkv)
     back_norm1, grad_norm1_part = norm_backward(resid_in, inv_rms1, gain1, back_normed1)
     back_tokens = back_middle + back_norm1
-    grad_norm1, grad_qkv, grad_bias, grad_out, grad_norm2 = (
-        lax.psum_scatter(
-            grad_norm1_part.astype(jnp.bfloat16), "group", scatter_dimension=0, tiled=True
-        ).astype(jnp.float32),
-        lax.psum_scatter(
-            grad_qkv_part.astype(jnp.bfloat16), "group", scatter_dimension=0, tiled=True
-        ).astype(jnp.float32),
-        lax.psum_scatter(
-            grad_bias_part.astype(jnp.bfloat16), "group", scatter_dimension=0, tiled=True
-        ).astype(jnp.float32),
-        lax.psum_scatter(
-            grad_out_part.astype(jnp.bfloat16), "group", scatter_dimension=0, tiled=True
-        ).astype(jnp.float32),
-        lax.psum_scatter(
-            grad_norm2_part.astype(jnp.bfloat16), "group", scatter_dimension=0, tiled=True
-        ).astype(jnp.float32),
-    )
-    grad_norm1, grad_qkv, grad_bias, grad_out, grad_norm2, grad_gate, grad_up, grad_down = (
-        lax.psum(grad_norm1.astype(jnp.bfloat16), "replica").astype(jnp.float32),
-        lax.psum(grad_qkv.astype(jnp.bfloat16), "replica").astype(jnp.float32),
-        lax.psum(grad_bias.astype(jnp.bfloat16), "replica").astype(jnp.float32),
-        lax.psum(grad_out.astype(jnp.bfloat16), "replica").astype(jnp.float32),
-        lax.psum(grad_norm2.astype(jnp.bfloat16), "replica").astype(jnp.float32),
-        lax.psum(grad_gate.astype(jnp.bfloat16), "replica").astype(jnp.float32),
-        lax.psum(grad_up.astype(jnp.bfloat16), "replica").astype(jnp.float32),
-        lax.psum(grad_down.astype(jnp.bfloat16), "replica").astype(jnp.float32),
+    small = jnp.stack([v.reshape(pairs, -1) for v in (grad_norm1_part, grad_norm2_part)], axis=1)
+    small = jnp.concatenate(
+        [small.reshape(pairs, -1), grad_bias_part.reshape(pairs, -1)], axis=1
+    ).reshape(-1)
+    small = scatter_owned(small, pairs)
+    owned = sum_owned(
+        small,
+        scatter_owned(grad_qkv_part, pairs),
+        scatter_owned(grad_out_part, pairs),
+        grad_gate,
+        grad_up,
+        grad_down,
+        copies,
+    )
+    small, grad_qkv, grad_out, grad_gate, grad_up, grad_down = (
+        a.astype(jnp.float32) for a in owned
+    )
+    gains = norm1_gain.shape[0]
+    grad_norm1, grad_norm2, grad_bias = (
+        small[:gains],
+        small[gains : 2 * gains],
+        small[2 * gains :],
     )
     shape_out = (sequences, length, model_width)
     return (
@@ -272,6 +499,9 @@
         P(None, "group"),
         P("group", None),
     )
+    program = functools.partial(
+        on_device, pairs=mesh.shape["group"], copies=mesh.shape["replica"]
+    )
     return jax.shard_map(
-        on_device, mesh=mesh, in_specs=in_specs, out_specs=out_specs, check_vma=False
-    )
+        program, mesh=mesh, in_specs=in_specs, out_specs=out_specs, check_vma=False
+    )

time: 506 us -> 394 us (0.78)
  waiting for transfers between devices: 332 us -> 52.7 us
  Pallas kernels: 0 us -> 210 us
  blocking collectives: 68.2 us -> 0 us
  local copies, waits for them, and re-layouts: 7.93 us -> 27.4 us
  between operations: 17.6 us -> 1.49 us
  starting transfers between devices: 0.76 us -> 13.5 us
  other arithmetic: 29.5 us -> 38.9 us
    psum x1 -> x0, waiting for transfers between devices: 232 us -> none  [on_device(): lax.psum(grad_qkv.astype(jnp.bfloat16), 'replica').astype(jnp.float32)]
    pallas_call x0 -> x1, Pallas kernels: none -> 210 us  [replica_sum(): pl.pallas_call(functools.partial(sum_kernel, copies, tuple(pieces), count...]
    reduce_scatter x4 -> x0, waiting for transfers between devices: 59.8 us -> none  [the longest x1 34.2 us: on_device(): lax.psum_scatter(grad_qkv_part.astype(jnp.bfloat16), 'group', scatter_dim...]
    ppermute x0 -> x12, waiting for transfers between devices: none -> 52.7 us  [the longest x10 51.6 us: swap(): return lax.ppermute(values, 'group', [(0, 1), (1, 0)])]
    all_gather x2 -> x0, waiting for transfers between devices: 38.2 us -> none  [the longest x1 23.2 us: on_device(): lax.all_gather(out_weight, 'group', axis=0, tiled=True)]
    psum x1 -> x0, blocking collectives: 33.8 us -> none  [on_device(): lax.psum(grad_norm1.astype(jnp.bfloat16), 'replica').astype(jnp.float32)]
    all_gather x2 -> x0, blocking collectives: 23.5 us -> none  [the longest x1 14.6 us: on_device(): lax.all_gather(back_rows, 'group', axis=0, tiled=True)]
    ppermute x0 -> x12, starting transfers between devices: none -> 13.5 us  [the longest x10 13 us: swap(): return lax.ppermute(values, 'group', [(0, 1), (1, 0)])]
  transfers between devices with their start and end apart: 7 -> 12, of which waited for: 7 -> 5; matrix products, arithmetic and copies ran while one was open for 9% -> 11% of each run, Pallas kernels for 0% -> 0%
where the time goes in v1:
time: 394 us; the launch traced here: 393 us
  Pallas kernels  210 us (53%)
  waiting for transfers between devices  52.7 us (13%)
  matrix products  48.7 us (12%)
  other arithmetic  38.9 us (10%)
  local copies, waits for them, and re-layouts  27.4 us (7%)
  starting transfers between devices  13.5 us (3%)
    pallas_call x1, Pallas kernels, replica_sum(): pl.pallas_call(functools.partial(sum_kernel, copies, tuple(pieces), count...  210 us
    ppermute x10, waiting for transfers between devices, swap(): return lax.ppermute(values, 'group', [(0, 1), (1, 0)])  51.6 us
    dot_general x5, matrix products, outer_sum(): lax.dot_general(left, right, (((0,), (0,)), ((), ())), preferred_element_...  19.8 us
    convert_element_type x6, other arithmetic, on_device(): a.astype(jnp.float32)  15.9 us
    ppermute x10, starting transfers between devices, swap(): return lax.ppermute(values, 'group', [(0, 1), (1, 0)])  13 us
    dot_general x5, matrix products, matmul(): return jnp.dot(left, right, preferred_element_type=jnp.float32)  12.9 us
    dot_general x5, matrix products, times_transposed(): lax.dot_general(left, right, (((1,), (1,)), ((), ())), preferred_element_...  11.7 us
    unnamed x104, local copies, waits for them, and re-layouts  8.23 us
  transfers between devices with their start and end apart: 12, of which 5 were waited for; matrix products, arithmetic and copies ran while one was open for 11% of the time, Pallas kernels for 0%

profile of v1, /device:TPU:0, one launch (start us, length us, event | category | flops | bytes accessed | tf_op | source)
XLA Modules:
  0.0 393.1 jit_solution(1020987977923220608)
XLA Ops:
  0.7 1.2 constant_dynamic-slice_fusion.1
  1.9 3.0 collective-permute-start.1
  4.9 2.1 concatenate.90
  7.0 1.8 constant_dynamic-slice_fusion
  8.8 2.0 collective-permute-start.3
  10.8 1.0 select_reduce_fusion
  11.8 0.8 select_compare_fusion
  13.8 3.8 collective-permute-done
  17.6 7.9 %collective-permute-done.3 = bf16[224,896]{1,0:T(8,128)(2,1)} collective-permute-done((bf16[224,896]{1,0:T(8,128)(2,1)}, bf16[224,896]{1,0:T(8,128)(2,1)}, u32[]{:S(2)}, u32[]{:S(2)}) %collective-permute-start.3) | collective-permute-done | bytes 401440 | tf_op jit(solution)/shard_map/ppermute | solution.py:233
  26.3 1.0 collective-permute-done.4
  27.4 1.1 broadcast_select_fusion.7
  28.5 1.4 broadcast_select_fusion.3
  30.5 0.6 convolution_add_fusion
  31.9 0.8 copy-done.22
  36.3 2.2 multiply_reduce_fusion.2
  38.5 0.8 multiply_convert_fusion.3
  39.3 1.7 collective-permute-start.5
  41.3 7.4 %collective-permute-done.5 = bf16[144,896]{1,0:T(8,128)(2,1)} collective-permute-done((bf16[144,896]{1,0:T(8,128)(2,1)}, bf16[144,896]{1,0:T(8,128)(2,1)}, u32[]{:S(2)}, u32[]{:S(2)}) %collective-permute-start.5) | collective-permute-done | bytes 258080 | tf_op jit(solution)/shard_map/ppermute | solution.py:233
  48.7 4.2 %fusion.52 = f32[288,2432]{1,0:T(8,128)S(1)} fusion(bf16[896,2432]{1,0:T(8,128)(2,1)} %param.19, bf16[144,896]{1,0:T(8,128)(2,1)} %collective-permute-done.5, bf16[144,896]{1,0:T(8,128)(2,1)} %multiply_convert_fusion.3), kind=kOutput, calls=%fused_computation.146 | convolution fusion | flops 1256177664 | bytes 7675904 | tf_op jit(solution)/shard_map/dot_general | solution.py:66
  52.9 4.3 %fusion.53 = f32[288,2432]{1,0:T(8,128)S(1)} fusion(bf16[896,2432]{1,0:T(8,128)(2,1)} %param.18, bf16[144,896]{1,0:T(8,128)(2,1)} %collective-permute-done.5, bf16[144,896]{1,0:T(8,128)(2,1)} %multiply_convert_fusion.3), kind=kOutput, calls=%fused_computation.147 | convolution fusion | flops 1256177664 | bytes 7675904 | tf_op jit(solution)/shard_map/dot_general | solution.py:66
  57.2 4.8 %multiply_convert_fusion = (bf16[288,2432]{1,0:T(8,128)(2,1)S(1)}, bf16[288,2432]{1,0:T(8,128)(2,1)S(1)}, bf16[288,2432]{1,0:T(8,128)(2,1)S(1)}) fusion(f32[288,2432]{1,0:T(8,128)S(1)} %fusion.53, f32[288,2432]{1,0:T(8,128)S(1)} %fusion.52, bf16[2432,896]{1,0:T(8,128)(2,1)} %param.20, bf16[144,896]{1,0:T(8,128)(2,1)S(1)} %collective-permute-done.7, ...), kind=kOutput, calls=%fused_computation.8 | convolution fusion | flops 1266683904 | bytes 14680064 | tf_op jit(solution)/shard_map/dot_general | solution.py:76
  62.2 1.9 fusion.61
  64.1 1.7 convolution_add_fusion.1
  65.9 1.8 collective-permute-start.8
  67.7 1.7 fusion.60
  69.7 5.7 %convolution_convert_fusion.1 = bf16[896,2432]{1,0:T(8,128)(2,1)} fusion(bf16[288,2432]{1,0:T(8,128)(2,1)S(1)} %get-tuple-element.22, bf16[144,896]{1,0:T(8,128)(2,1)} %collective-permute-done.5, bf16[144,896]{1,0:T(8,128)(2,1)} %multiply_convert_fusion.3), kind=kOutput, calls=%fused_computation.1 | convolution fusion | flops 1258356736 | bytes 6275072 | tf_op jit(solution)/shard_map/dot_general | solution.py:70
  75.4 5.7 %convolution_convert_fusion.2 = bf16[896,2432]{1,0:T(8,128)(2,1)} fusion(bf16[288,2432]{1,0:T(8,128)(2,1)S(1)} %get-tuple-element.23, bf16[144,896]{1,0:T(8,128)(2,1)} %collective-permute-done.5, bf16[144,896]{1,0:T(8,128)(2,1)} %multiply_convert_fusion.3), kind=kOutput, calls=%fused_computation.2 | convolution fusion | flops 1258356736 | bytes 6275072 | tf_op jit(solution)/shard_map/dot_general | solution.py:70
  81.1 5.6 %convolution_convert_fusion = bf16[2432,896]{1,0:T(8,128)(2,1)} fusion(bf16[288,2432]{1,0:T(8,128)(2,1)S(1)} %get-tuple-element.24, bf16[144,896]{1,0:T(8,128)(2,1)S(1)} %copy-done.38, bf16[144,896]{1,0:T(8,128)(2,1)} %bitcast.17), kind=kOutput, calls=%fused_computation | convolution fusion | flops 1258356736 | bytes 6275072 | tf_op jit(solution)/shard_map/dot_general | solution.py:70
  86.8 0.8 multiply_reduce_fusion
  87.6 2.0 subtract_add_fusion
  89.6 0.8 copy-done.3
  91.8 0.6 fusion.10
  93.6 1.1 convolution_bitcast_fusion
  94.7 1.1 fusion.27
  95.9 0.6 fusion.32
  96.5 1.0 fusion.55
  97.5 2.5 copy.90
  100.1 2.5 copy.91
  102.6 1.9 multiply_add_fusion
  104.5 1.4 pad_maximum_fusion.5
  105.9 2.4 reshape.511
  108.3 0.9 multiply_add_fusion.1
  109.2 0.7 pad_maximum_fusion.19
  109.9 1.0 copy.73
  110.9 1.6 copy.74
  112.5 2.1 fusion.35
  114.7 2.6 fusion.21
  117.4 1.1 dynamic-slice_convert_fusion
  118.5 1.7 collective-permute-start.9
  120.3 1.0 dynamic-slice_convert_fusion.1
  122.1 1.7 collective-permute-start.11
  123.8 2.3 fusion.18
  126.1 32.6 %collective-permute-done.11 = bf16[1472]{0:T(1024)(128)(2,1)S(1)} collective-permute-done((bf16[1472]{0:T(1024)(128)(2,1)S(1)}, bf16[1472]{0:T(1024)(128)(2,1)S(1)}, u32[]{:S(2)}, u32[]{:S(2)}) %collective-permute-start.11) | collective-permute-done | bytes 2976 | tf_op jit(solution)/shard_map/ppermute | solution.py:233
  158.9 1.3 add_convert_fusion.1
  160.2 1.5 add_convert_fusion
  162.1 1.5 pad_maximum_fusion
  163.6 210.5 %replica_sum.1 = (bf16[16,56,2432]{2,1,0:T(8,128)(2,1)}, bf16[16,56,2432]{2,1,0:T(8,128)(2,1)}, bf16[16,152,896]{2,1,0:T(8,128)(2,1)}, bf16[16,64,1024]{2,1,0:T(8,128)(2,1)}) custom-call(bf16[16,56,2432]{2,1,0:T(8,128)(2,1)} %bitcast.138, bf16[16,56,2432]{2,1,0:T(8,128)(2,1)} %bitcast.137, bf16[16,152,896]{2,1,0:T(8,128)(2,1)} %bitcast.139, ...), custom_call_target="tpu_custom_call" | custom-call | tf_op jit(solution)/shard_map/replica_sum/pallas_call | solution.py:212
  374.1 1.9 fusion.54
  376.0 1.3 slice_convert_fusion
  377.3 1.4 fusion.11
  378.7 0.7 fusion.56
  380.0 4.4 %bitcast_convert_fusion = f32[2432,896]{1,0:T(8,128)} fusion(bf16[16,152,896]{2,1,0:T(8,128)(2,1)S(1)} %bitcast.136), kind=kLoop, calls=%fused_computation.3 | loop fusion | flops 2179072 | bytes 13074432 | tf_op jit(solution)/shard_map/convert_element_type | solution.py:453
  384.4 4.4 %bitcast_convert_fusion.1 = f32[896,2432]{1,0:T(8,128)} fusion(bf16[16,56,2432]{2,1,0:T(8,128)(2,1)S(1)} %bitcast.134), kind=kLoop, calls=%fused_computation.4 | loop fusion | flops 2179072 | bytes 13074432 | tf_op jit(solution)/shard_map/convert_element_type | solution.py:453
  388.8 4.4 %bitcast_convert_fusion.2 = f32[896,2432]{1,0:T(8,128)} fusion(bf16[16,56,2432]{2,1,0:T(8,128)(2,1)S(1)} %bitcast.132), kind=kLoop, calls=%fused_computation.5 | loop fusion | flops 2179072 | bytes 13074432 | tf_op jit(solution)/shard_map/convert_element_type | solution.py:453
  (175 shorter events, 12.3 us)
Async XLA Ops:
  0.6 12.0 %copy-start.6 = (bf16[1,144,896]{2,1,0:T(8,128)(2,1)S(1)}, bf16[1,144,896]{2,1,0:T(8,128)(2,1)}, u32[]{:S(2)}) copy-start(bf16[1,144,896]{2,1,0:T(8,128)(2,1)} %param.11) | copy-start | bytes 774148
  0.7 27.8 %copy-start.9 = (bf16[448,896]{1,0:T(8,128)(2,1)S(1)}, bf16[448,896]{1,0:T(8,128)(2,1)}, u32[]{:S(2)}) copy-start(bf16[448,896]{1,0:T(8,128)(2,1)} %param.16) | copy-start | bytes 2408452
  1.9 24.0 %collective-permute-start.1 = (bf16[224,1152]{1,0:T(8,128)(2,1)S(1)}, bf16[224,1152]{1,0:T(8,128)(2,1)S(1)}, u32[]{:S(2)}, u32[]{:S(2)}) collective-permute-start(bf16[224,1152]{1,0:T(8,128)(2,1)S(1)} %constant_dynamic-slice_fusion.1), channel_id=1, source_target_pairs={{0,16},{16,0},{1,17},{17,1},{2,18},{18,2},{3,19},{19,3},{4,20},{20... | collective-permute-start | bytes 1548296 | tf_op jit(solution)/shard_map/ppermute | solution.py:233
  7.0 10.5 %collective-permute-start = (bf16[1472]{0:T(1024)(128)(2,1)S(1)}, bf16[1472]{0:T(1024)(128)(2,1)S(1)}, u32[]{:S(2)}, u32[]{:S(2)}) collective-permute-start(bf16[1472]{0:T(1024)(128)(2,1)S(1)} %concatenate.90), channel_id=1, source_target_pairs={{0,16},{16,0},{1,17},{17,1},{2,18},{18,2},{3,19},{19,3},{4,20},{20... | collective-permute-start | bytes 8840 | tf_op jit(solution)/shard_map/ppermute | solution.py:233
  8.8 16.6 %collective-permute-start.3 = (bf16[224,896]{1,0:T(8,128)(2,1)}, bf16[224,896]{1,0:T(8,128)(2,1)}, u32[]{:S(2)}, u32[]{:S(2)}) collective-permute-start(bf16[224,896]{1,0:T(8,128)(2,1)} %constant_dynamic-slice_fusion), channel_id=1, source_target_pairs={{0,16},{16,0},{1,17},{17,1},{2,18},{18,2},{3,19},{19,3},{4,20},{20... | collective-permute-start | bytes 1204232 | tf_op jit(solution)/shard_map/ppermute | solution.py:233
  13.0 21.6 %copy-start.23 = (f32[144,32]{0,1:T(8,128)}, f32[144,32]{0,1:T(8,128)S(1)}, u32[]{:S(2)}) copy-start(f32[144,32]{0,1:T(8,128)S(1)} %get-tuple-element.57) | copy-start | bytes 55300
  13.0 21.6 %copy-start.25 = (f32[144,32]{0,1:T(8,128)}, f32[144,32]{0,1:T(8,128)S(1)}, u32[]{:S(2)}) copy-start(f32[144,32]{0,1:T(8,128)S(1)} %get-tuple-element.58) | copy-start | bytes 55300
  13.6 101.0 %copy-start.32 = (f32[144]{0:T(256)}, f32[144]{0:T(256)S(1)}, u32[]{:S(2)}) copy-start(f32[144]{0:T(256)S(1)} %get-tuple-element.60) | copy-start | bytes 1732
  13.8 19.2 %copy-start.21 = (f32[144,32]{1,0:T(8,128)}, f32[144,32]{1,0:T(8,128)S(1)}, u32[]{:S(2)}) copy-start(f32[144,32]{1,0:T(8,128)S(1)} %copy.60) | copy-start | bytes 55300
  25.4 1.9 collective-permute-start.4
  25.8 4.1 %collective-permute-start.2 = (bf16[224,1152]{1,0:T(8,128)(2,1)S(1)}, bf16[224,1152]{1,0:T(8,128)(2,1)S(1)}, u32[]{:S(2)}, u32[]{:S(2)}) collective-permute-start(bf16[224,1152]{1,0:T(8,128)(2,1)S(1)} %collective-permute-done.1), channel_id=1, source_target_pairs={{0,1},{1,0},{2,3},{3,2},{4,5},{5,4},{6,7},{7,6},{8,9},{9,8},{10,11... | collective-permute-start | bytes 1548296 | tf_op jit(solution)/shard_map/ppermute | solution.py:242
  28.5 1.6 copy-start.5
  30.4 1.0 copy-start.10
  30.5 1.4 copy-start.12
  31.8 0.8 copy-start.22
  33.0 1.5 slice-start.6
  34.0 1.5 copy-start.14
  34.5 1.1 copy-start.16
  34.6 0.9 copy-start.27
  34.7 0.9 copy-start.29
  36.3 3.0 copy-start.7
  39.3 9.4 %collective-permute-start.5 = (bf16[144,896]{1,0:T(8,128)(2,1)}, bf16[144,896]{1,0:T(8,128)(2,1)}, u32[]{:S(2)}, u32[]{:S(2)}) collective-permute-start(bf16[144,896]{1,0:T(8,128)(2,1)} %multiply_convert_fusion.3), channel_id=1, source_target_pairs={{0,16},{16,0},{1,17},{17,1},{2,18},{18,2},{3,19},{19,3},{4,20},{20... | collective-permute-start | bytes 774152 | tf_op jit(solution)/shard_map/ppermute | solution.py:233
  41.1 16.2 %collective-permute-start.7 = (bf16[144,896]{1,0:T(8,128)(2,1)}, bf16[144,896]{1,0:T(8,128)(2,1)S(1)}, u32[]{:S(2)}, u32[]{:S(2)}) collective-permute-start(bf16[144,896]{1,0:T(8,128)(2,1)} %bitcast.17), channel_id=1, source_target_pairs={{0,16},{16,0},{1,17},{17,1},{2,18},{18,2},{3,19},{19,3},{4,20},{20... | collective-permute-start | bytes 774152 | tf_op jit(solution)/shard_map/ppermute | solution.py:233
  52.9 9.2 %slice-start.7 = ((s8[4358144]{0:T(1024)(128)(4,1)}), s8[4194304]{0:T(1024)(128)(4,1)S(1)}, s32[]{:S(2)}) async-start(s8[4358144]{0:T(1024)(128)(4,1)} %bitcast.157), calls=%async_computation.7 | async-start | bytes 8388608
  52.9 11.2 %slice-start.9 = ((s8[4358144]{0:T(1024)(128)(4,1)}), s8[4194304]{0:T(1024)(128)(4,1)S(1)}, s32[]{:S(2)}) async-start(s8[4358144]{0:T(1024)(128)(4,1)} %bitcast.159), calls=%async_computation.9 | async-start | bytes 8388608
  57.2 4.9 %slice-start.8 = ((s8[4358144]{0:T(1024)(128)(4,1)}), s8[163840]{0:T(1024)(128)(4,1)S(1)}, s32[]{:S(2)}) async-start(s8[4358144]{0:T(1024)(128)(4,1)} %bitcast.157), calls=%async_computation.8 | async-start | bytes 327680
  57.2 6.8 %slice-start.10 = ((s8[4358144]{0:T(1024)(128)(4,1)}), s8[163840]{0:T(1024)(128)(4,1)S(1)}, s32[]{:S(2)}) async-start(s8[4358144]{0:T(1024)(128)(4,1)} %bitcast.159), calls=%async_computation.10 | async-start | bytes 327680
  57.2 4.9 %copy-start.37 = (bf16[144,896]{1,0:T(8,128)(2,1)}, bf16[144,896]{1,0:T(8,128)(2,1)S(1)}, u32[]{:S(2)}) copy-start(bf16[144,896]{1,0:T(8,128)(2,1)S(1)} %collective-permute-done.7) | copy-start | bytes 774148
  62.1 5.5 %slice-start.11 = ((s8[4358144]{0:T(1024)(128)(4,1)}), s8[4194304]{0:T(1024)(128)(4,1)S(1)}, s32[]{:S(2)}) async-start(s8[4358144]{0:T(1024)(128)(4,1)} %bitcast.161), calls=%async_computation.11 | async-start | bytes 8388608
  64.1 3.6 slice-start.12
  65.9 20.9 %collective-permute-start.8 = (bf16[144,896]{1,0:T(8,128)(2,1)S(1)}, bf16[144,896]{1,0:T(8,128)(2,1)S(1)}, u32[]{:S(2)}, u32[]{:S(2)}) collective-permute-start(bf16[144,896]{1,0:T(8,128)(2,1)S(1)} %slice.207), channel_id=1, source_target_pairs={{0,16},{16,0},{1,17},{17,1},{2,18},{18,2},{3,19},{19,3},{4,20},{20... | collective-permute-start | bytes 774152 | tf_op jit(solution)/shard_map/ppermute | solution.py:233
  69.4 18.2 %collective-permute-start.6 = (bf16[144,896]{1,0:T(8,128)(2,1)S(1)}, bf16[144,896]{1,0:T(8,128)(2,1)S(1)}, u32[]{:S(2)}, u32[]{:S(2)}) collective-permute-start(bf16[144,896]{1,0:T(8,128)(2,1)S(1)} %slice.208), channel_id=1, source_target_pairs={{0,16},{16,0},{1,17},{17,1},{2,18},{18,2},{3,19},{19,3},{4,20},{20... | collective-permute-start | bytes 774152 | tf_op jit(solution)/shard_map/ppermute | solution.py:233
  75.4 5.7 %copy-start.38 = (bf16[144,896]{1,0:T(8,128)(2,1)S(1)}, bf16[144,896]{1,0:T(8,128)(2,1)}, u32[]{:S(2)}) copy-start(bf16[144,896]{1,0:T(8,128)(2,1)} %copy-done.37) | copy-start | bytes 774148
  86.8 3.6 copy-start.18
  86.8 3.6 copy-start.19
  89.6 0.8 copy-start.3
  91.8 0.8 copy-start.28
  91.8 0.8 copy-start.30
  92.6 0.9 copy-start.15
  92.6 1.0 copy-start.17
  93.6 2.3 copy-start.4
  93.6 2.3 copy-start.8
  104.5 3.8 copy-start.24
  104.5 3.8 copy-start.26
  112.5 2.1 copy-start.2
  112.5 2.1 copy-start.11
  112.5 2.1 copy-start.13
  112.5 2.2 copy-start.20
  114.7 2.7 copy-start
  117.4 4.1 %copy-start.35 = (f32[896]{0:T(1024)S(1)}, f32[896]{0:T(1024)}, u32[]{:S(2)}) copy-start(f32[896]{0:T(1024)} %get-tuple-element.20) | copy-start | bytes 10756
  117.4 4.2 %copy-start.31 = (f32[896]{0:T(1024)S(1)}, f32[896]{0:T(1024)}, u32[]{:S(2)}) copy-start(f32[896]{0:T(1024)} %get-tuple-element.18) | copy-start | bytes 10756
  117.4 6.4 %copy-start.36 = (f32[144]{0:T(256)S(1)}, f32[144]{0:T(256)}, u32[]{:S(2)}) copy-start(f32[144]{0:T(256)} %get-tuple-element.21) | copy-start | bytes 1732
  117.4 6.4 %copy-start.33 = (f32[144]{0:T(256)S(1)}, f32[144]{0:T(256)}, u32[]{:S(2)}) copy-start(f32[144]{0:T(256)} %copy-done.32) | copy-start | bytes 1732
  117.4 6.4 %copy-start.34 = (f32[144]{0:T(256)S(1)}, f32[144]{0:T(256)}, u32[]{:S(2)}) copy-start(f32[144]{0:T(256)} %get-tuple-element.59) | copy-start | bytes 1732
  118.5 41.7 %collective-permute-start.9 = (bf16[448,1152]{1,0:T(8,128)(2,1)}, bf16[448,1152]{1,0:T(8,128)(2,1)}, u32[]{:S(2)}, u32[]{:S(2)}) collective-permute-start(bf16[448,1152]{1,0:T(8,128)(2,1)} %dynamic-slice_convert_fusion), channel_id=1, source_target_pairs={{0,16},{16,0},{1,17},{17,1},{2,18},{18,2},{3,19},{19,3},{4,20},{20... | collective-permute-start | bytes 3096584 | tf_op jit(solution)/shard_map/ppermute | solution.py:233
  121.2 37.6 %collective-permute-start.10 = (bf16[448,896]{1,0:T(8,128)(2,1)}, bf16[448,896]{1,0:T(8,128)(2,1)}, u32[]{:S(2)}, u32[]{:S(2)}) collective-permute-start(bf16[448,896]{1,0:T(8,128)(2,1)} %dynamic-slice_convert_fusion.1), channel_id=1, source_target_pairs={{0,16},{16,0},{1,17},{17,1},{2,18},{18,2},{3,19},{19,3},{4,20},{20... | collective-permute-start | bytes 2408456 | tf_op jit(solution)/shard_map/ppermute | solution.py:233
  122.1 36.7 %collective-permute-start.11 = (bf16[1472]{0:T(1024)(128)(2,1)S(1)}, bf16[1472]{0:T(1024)(128)(2,1)S(1)}, u32[]{:S(2)}, u32[]{:S(2)}) collective-permute-start(bf16[1472]{0:T(1024)(128)(2,1)S(1)} %dynamic_slice.43), channel_id=1, source_target_pairs={{0,16},{16,0},{1,17},{17,1},{2,18},{18,2},{3,19},{19,3},{4,20},{20... | collective-permute-start | bytes 8840 | tf_op jit(solution)/shard_map/ppermute | solution.py:233
  123.8 36.4 %copy-start.1 = (f32[896,1152]{1,0:T(8,128)S(1)}, f32[896,1152]{1,0:T(8,128)}, u32[]{:S(2)}) copy-start(f32[896,1152]{1,0:T(8,128)} %copy-done) | copy-start | bytes 12386308
  374.1 5.9 %slice-start.4 = ((s8[4358144]{0:T(1024)(128)(4,1)}), s8[4194304]{0:T(1024)(128)(4,1)S(1)}, s32[]{:S(2)}) async-start(s8[4358144]{0:T(1024)(128)(4,1)} %bitcast.135), calls=%async_computation.4 | async-start | bytes 8388608
  376.0 4.0 %slice-start.5 = ((s8[4358144]{0:T(1024)(128)(4,1)}), s8[163840]{0:T(1024)(128)(4,1)S(1)}, s32[]{:S(2)}) async-start(s8[4358144]{0:T(1024)(128)(4,1)} %bitcast.135), calls=%async_computation.5 | async-start | bytes 327680
  378.7 5.7 %slice-start.2 = ((s8[4358144]{0:T(1024)(128)(4,1)}), s8[4194304]{0:T(1024)(128)(4,1)S(1)}, s32[]{:S(2)}) async-start(s8[4358144]{0:T(1024)(128)(4,1)} %bitcast.133), calls=%async_computation.2 | async-start | bytes 8388608
  380.0 4.4 %slice-start.3 = ((s8[4358144]{0:T(1024)(128)(4,1)}), s8[163840]{0:T(1024)(128)(4,1)S(1)}, s32[]{:S(2)}) async-start(s8[4358144]{0:T(1024)(128)(4,1)} %bitcast.133), calls=%async_computation.3 | async-start | bytes 327680
  380.0 8.8 %slice-start = ((s8[4358144]{0:T(1024)(128)(4,1)}), s8[4194304]{0:T(1024)(128)(4,1)S(1)}, s32[]{:S(2)}) async-start(s8[4358144]{0:T(1024)(128)(4,1)} %bitcast.131), calls=%async_computation | async-start | bytes 8388608
  384.4 4.4 %slice-start.1 = ((s8[4358144]{0:T(1024)(128)(4,1)}), s8[163840]{0:T(1024)(128)(4,1)S(1)}, s32[]{:S(2)}) async-start(s8[4358144]{0:T(1024)(128)(4,1)} %bitcast.131), calls=%async_computation.1 | async-start | bytes 327680

commit v2 on v1

--- a/solution.py
+++ b/solution.py
@@ -93,137 +93,156 @@
     return bits
 
 
-def sum_kernel(copies, pieces, count, *refs):
+def sum_kernel(copies, pieces, swapped, count, *refs):
     ins, outs = refs[:count], refs[count : 2 * count]
     n = len(pieces)
     held = refs[2 * count : 2 * count + n]
     landed = refs[2 * count + n : 2 * count + 2 * n]
     final = refs[2 * count + 2 * n : 2 * count + 3 * n]
-    send_sem, recv_sem, local_sem = refs[2 * count + 3 * n :]
+    extra = refs[2 * count + 3 * n : -3]
+    send_sem, recv_sem, local_sem = refs[-3:]
     me = lax.axis_index("replica")
+    pair = lax.axis_index("group")
     stages = copies.bit_length() - 1
+    mesh_id = pl.DeviceIdType.MESH
 
     def partner(bit):
         return me + bit * (1 - 2 * (lax.div(me, bit) % 2))
 
     loads = []
-    for p, (which, start, width, _) in enumerate(pieces):
+    for p, (which, start, width, _, _) in enumerate(pieces):
+        source = ins[which].at[pair] if which == swapped else ins[which]
         load = pltpu.make_async_copy(
-            ins[which].at[:, :, pl.ds(start, width)], held[p], local_sem.at[p, 0]
+            source.at[:, :, pl.ds(start, width)], held[p], local_sem.at[p, 0]
         )
         load.start()
         loads.append(load)
     barrier = pltpu.get_barrier_semaphore()
     for i in range(stages):
         pl.semaphore_signal(
-            barrier,
-            inc=1,
-            device_id={"replica": partner(1 << i)},
-            device_id_type=pl.DeviceIdType.MESH,
+            barrier, inc=1, device_id={"replica": partner(1 << i)}, device_id_type=mesh_id
         )
-    pl.semaphore_wait(barrier, stages)
-
-    bits = [stage_bits(copies, far) for (_, _, _, far) in pieces]
+    pl.semaphore_signal(barrier, inc=1, device_id={"group": 1 - pair}, device_id_type=mesh_id)
+    pl.semaphore_wait(barrier, stages + 1)
+
+    swaps, at = {}, 0
+    for p, (which, start, width, _, _) in enumerate(pieces):
+        if which == swapped:
+            copy = pltpu.make_async_remote_copy(
+                src_ref=ins[which].at[1 - pair].at[:, :, pl.ds(start, width)],
+                dst_ref=extra[at],
+                send_sem=send_sem.at[p, 2 * stages],
+                recv_sem=recv_sem.at[p, 2 * stages],
+                device_id={"group": 1 - pair},
+                device_id_type=mesh_id,
+            )
+            copy.start()
+            swaps[p] = (copy, extra[at])
+            at += 1
+
+    bits = [stage_bits(copies, far) for (_, _, _, far, _) in pieces]
     base = [0] * n
     trail = [[] for _ in range(n)]
     copying = [None] * n
-    for k in range(stages + 1):
+    stores = []
+
+    def accumulate(goal, left, right, first, shift, size):
+        def add(i, carry):
+            goal[first + i] = left[first + i] + right[shift + i]
+            return carry
+
+        lax.fori_loop(0, size, add, 0)
+
+    def spread(p, k):
+        block = final[p].at[pl.ds(trail[p][k], copies >> (k + 1))]
+        return pltpu.make_async_remote_copy(
+            src_ref=block,
+            dst_ref=block,
+            send_sem=send_sem.at[p, stages + k],
+            recv_sem=recv_sem.at[p, stages + k],
+            device_id={"replica": partner(bits[p][k])},
+            device_id_type=mesh_id,
+        )
+
+    def halve(p, k):
         size = copies >> (k + 1)
-        offset = copies - (copies >> k)
+        bit = bits[p][k]
+        side = lax.div(me, bit) % 2
+        keep, give = base[p] + side * size, base[p] + (1 - side) * size
+        trail[p].append(keep)
+        base[p] = keep
+        return pltpu.make_async_remote_copy(
+            src_ref=held[p].at[pl.ds(give, size)],
+            dst_ref=landed[p].at[pl.ds(copies - (copies >> k), size)],
+            send_sem=send_sem.at[p, k],
+            recv_sem=recv_sem.at[p, k],
+            device_id={"replica": partner(bit)},
+            device_id_type=mesh_id,
+        )
+
+    def step(p, k):
+        if k == 0:
+            loads[p].wait()
+            if p in swaps:
+                swaps[p][0].wait()
+                accumulate(held[p], held[p], swaps[p][1], 0, 0, copies)
+        else:
+            copying[p].wait()
+            if k <= stages:
+                goal = held[p] if k < stages else final[p]
+                shift = copies - (copies >> (k - 1))
+                accumulate(goal, held[p], landed[p], base[p], shift, copies >> k)
+        if k < stages:
+            copying[p] = halve(p, k)
+        elif k < 2 * stages:
+            copying[p] = spread(p, 2 * stages - 1 - k)
+        else:
+            which, start, width, _, _ = pieces[p]
+            store = pltpu.make_async_copy(
+                final[p], outs[which].at[:, :, pl.ds(start, width)], local_sem.at[p, 1]
+            )
+            store.start()
+            stores.append(store)
+            return
+        copying[p].start()
+
+    for tick in range(2 * stages + 1 + max(piece[4] for piece in pieces)):
         for p in range(n):
-            if k == 0:
-                loads[p].wait()
-            else:
-                copying[p].wait()
-                old, previous = copies >> k, copies - (copies >> (k - 1))
-                first = base[p]
-
-                goal = held[p] if k < stages else final[p]
-
-                def add(i, carry, p=p, goal=goal, first=first, previous=previous):
-                    goal[first + i] = held[p][first + i] + landed[p][previous + i]
-                    return carry
-
-                lax.fori_loop(0, old, add, 0)
-            if k < stages:
-                bit = bits[p][k]
-                side = lax.div(me, bit) % 2
-                keep, give = base[p] + side * size, base[p] + (1 - side) * size
-                copy = pltpu.make_async_remote_copy(
-                    src_ref=held[p].at[pl.ds(give, size)],
-                    dst_ref=landed[p].at[pl.ds(offset, size)],
-                    send_sem=send_sem.at[p, k],
-                    recv_sem=recv_sem.at[p, k],
-                    device_id={"replica": partner(bit)},
-                    device_id_type=pl.DeviceIdType.MESH,
-                )
-                trail[p].append(keep)
-                base[p] = keep
-            else:
-                copy = spread(final, send_sem, recv_sem, trail, bits, partner, p, k - 1, copies)
-            copy.start()
-            copying[p] = copy
-    stores = []
-    for k in range(stages - 1, -1, -1):
-        for p, (which, start, width, _) in enumerate(pieces):
-            copying[p].wait()
-            if k > 0:
-                copying[p] = spread(
-                    final, send_sem, recv_sem, trail, bits, partner, p, k - 1, copies
-                )
-                copying[p].start()
-            else:
-                store = pltpu.make_async_copy(
-                    final[p], outs[which].at[:, :, pl.ds(start, width)], local_sem.at[p, 1]
-                )
-                store.start()
-                stores.append(store)
+            k = tick - pieces[p][4]
+            if 0 <= k <= 2 * stages:
+                step(p, k)
     for store in stores:
         store.wait()
 
 
-def spread(final, send_sem, recv_sem, trail, bits, partner, p, k, copies):
-    block = final[p].at[pl.ds(trail[p][k], copies >> (k + 1))]
-    stages = copies.bit_length() - 1
-    return pltpu.make_async_remote_copy(
-        src_ref=block,
-        dst_ref=block,
-        send_sem=send_sem.at[p, stages + k],
-        recv_sem=recv_sem.at[p, stages + k],
-        device_id={"replica": partner(bits[p][k])},
-        device_id_type=pl.DeviceIdType.MESH,
-    )
-
-
 def replica_sum(arrays, copies):
+    swapped = len(arrays) - 1
     pieces = []
     for which, array in enumerate(arrays):
-        columns = array.shape[2]
-        cut = -(-columns // 256) * 128
-        if columns > 1024:
-            pieces += [(which, 0, cut, False), (which, cut, columns - cut, True)]
-        else:
-            half = columns // 256 * 128
-            pieces += [(which, 0, half, True), (which, half, columns - half, False)]
+        columns = array.shape[-1]
+        cut = columns // 256 * 128
+        pieces += [(which, 0, cut, False, which), (which, cut, columns - cut, True, which)]
     stages = copies.bit_length() - 1
     n, count = len(pieces), len(arrays)
-    shapes = [(arrays[w].shape[1], width) for (w, _, width, _) in pieces]
+    shapes = [(arrays[w].shape[-2], width) for (w, _, width, _, _) in pieces]
+    moved = [shape for shape, piece in zip(shapes, pieces) if piece[0] == swapped]
     any_spec = pl.BlockSpec(memory_space=pltpu.HBM)
     return pl.pallas_call(
-        functools.partial(sum_kernel, copies, tuple(pieces), count),
-        out_shape=[jax.ShapeDtypeStruct(a.shape, a.dtype) for a in arrays],
+        functools.partial(sum_kernel, copies, tuple(pieces), swapped, count),
+        out_shape=[jax.ShapeDtypeStruct(a.shape[-3:], a.dtype) for a in arrays],
         in_specs=[any_spec] * count,
         out_specs=[any_spec] * count,
         scratch_shapes=[pltpu.VMEM((copies, r, c), jnp.bfloat16) for r, c in shapes]
         + [pltpu.VMEM((copies - 1, r, c), jnp.bfloat16) for r, c in shapes]
         + [pltpu.VMEM((copies, r, c), jnp.bfloat16) for r, c in shapes]
+        + [pltpu.VMEM((copies, r, c), jnp.bfloat16) for r, c in moved]
         + [
-            pltpu.SemaphoreType.DMA((n, 2 * stages)),
-            pltpu.SemaphoreType.DMA((n, 2 * stages)),
+            pltpu.SemaphoreType.DMA((n, 2 * stages + 1)),
+            pltpu.SemaphoreType.DMA((n, 2 * stages + 1)),
             pltpu.SemaphoreType.DMA((n, 2)),
         ],
         compiler_params=pltpu.CompilerParams(
-            collective_id=0, has_side_effects=True, vmem_limit_bytes=52 * 1024 * 1024
+            collective_id=0, has_side_effects=True, vmem_limit_bytes=54 * 1024 * 1024
         ),
         name="replica_sum",
     )(*arrays)
@@ -279,39 +298,37 @@
     return partial[:half] + swap(partial[half:].astype(jnp.bfloat16)).astype(jnp.float32)
 
 
-def scatter_owned(partial, pairs):
-    if pairs != 2:
-        return lax.psum_scatter(
-            partial.astype(jnp.bfloat16), "group", scatter_dimension=0, tiled=True
-        ).astype(jnp.float32)
-    half = partial.shape[0] // 2
-    me = lax.axis_index("group")
-    give = lax.dynamic_slice_in_dim(partial.astype(jnp.bfloat16), (1 - me) * half, half, 0)
-    keep = lax.dynamic_slice_in_dim(partial, me * half, half, 0)
-    return keep + swap(give).astype(jnp.float32)
-
-
-def sum_owned(small, qkv, out, gate, up, down, copies):
-    rows, width = qkv.shape[0], qkv.shape[1] + out.shape[1]
+def scatter_owned(partial):
+    return lax.psum_scatter(
+        partial.astype(jnp.bfloat16), "group", scatter_dimension=0, tiled=True
+    ).astype(jnp.float32)
+
+
+def sum_owned(small, qkv, out, gate, up, down, pairs, copies):
+    rows, width = qkv.shape[0] // pairs, qkv.shape[1] + out.shape[1]
+    share = small.shape[0] // pairs
     lines = 64
     fits = (
         copies == 16
+        and pairs == 2
         and width % 256 == 0
-        and rows + 64 == copies // 2 * 64
-        and small.shape[0] <= width
+        and rows + lines == copies // 2 * lines
+        and share <= width
         and all(a.shape[0] % (8 * copies) == 0 and a.shape[1] % 128 == 0 for a in (gate, up, down))
     )
     if not fits:
+        owned = [scatter_owned(a) for a in (small, qkv, out)]
         return lax.psum(
-            tuple(a.astype(jnp.bfloat16) for a in (small, qkv, out, gate, up, down)), "replica"
+            tuple(a.astype(jnp.bfloat16) for a in (*owned, gate, up, down)), "replica"
         )
-    joined = jnp.concatenate([qkv, out], axis=1)
-    line = jnp.pad(small, (0, width - small.shape[0]))[None, :]
-    joined = jnp.concatenate(
-        [joined, jnp.pad(line, ((0, lines - 1), (0, 0)))], axis=0
-    ).astype(jnp.bfloat16)
     half = width // 2
-    joined = jnp.stack([joined[:, :half], joined[:, half:]]).reshape(copies, lines, half)
+    joined = jnp.concatenate([qkv, out], axis=1).astype(jnp.bfloat16)
+    joined = jnp.stack([joined[:, :half], joined[:, half:]])
+    joined = joined.reshape(2, pairs, rows // lines, lines, half).transpose(1, 0, 2, 3, 4)
+    small = small.astype(jnp.bfloat16).reshape(pairs, share)
+    line = jnp.pad(small, ((0, 0), (0, width - share))).reshape(pairs, 2, 1, 1, half)
+    line = jnp.pad(line, ((0, 0), (0, 0), (0, 0), (0, lines - 1), (0, 0)))
+    joined = jnp.concatenate([joined, line], axis=2).reshape(pairs, copies, lines, half)
     folded = [
         a.astype(jnp.bfloat16).reshape(copies, a.shape[0] // copies, a.shape[1])
         for a in (gate, up, down)
@@ -320,7 +337,7 @@
     joined = joined.reshape(2, rows + lines, half)
     joined = jnp.concatenate([joined[0], joined[1]], axis=1)
     return (
-        joined[rows, : small.shape[0]],
+        joined[rows, :share],
         joined[:rows, : qkv.shape[1]],
         joined[:rows, qkv.shape[1] :],
         gate_s.reshape(gate.shape),
@@ -439,14 +456,14 @@
     small = jnp.concatenate(
         [small.reshape(pairs, -1), grad_bias_part.reshape(pairs, -1)], axis=1
     ).reshape(-1)
-    small = scatter_owned(small, pairs)
     owned = sum_owned(
         small,
-        scatter_owned(grad_qkv_part, pairs),
-        scatter_owned(grad_out_part, pairs),
+        grad_qkv_part,
+        grad_out_part,
         grad_gate,
         grad_up,
         grad_down,
+        pairs,
         copies,
     )
     small, grad_qkv, grad_out, grad_gate, grad_up, grad_down = (

time: 394 us -> 322 us (0.82)
  waiting for transfers between devices: 52.7 us -> 20.8 us
  local copies, waits for them, and re-layouts: 27.4 us -> 15.9 us
  matrix products: 48.7 us -> 39.3 us
  other arithmetic: 38.9 us -> 31.1 us
  Pallas kernels: 210 us -> 203 us
    ppermute x10 -> x7, waiting for transfers between devices: 51.6 us -> 19.9 us  [swap(): return lax.ppermute(values, 'group', [(0, 1), (1, 0)])]
    pallas_call x1, Pallas kernels: 210 us -> 203 us  [replica_sum(): pl.pallas_call(functools.partial(sum_kernel, copies, tuple(pieces), swapp...]
    dot_general x5, matrix products: 12.9 us -> 6.22 us  [matmul(): return jnp.dot(left, right, preferred_element_type=jnp.float32)]
    another operation x6 -> x2, other arithmetic: 5.5 us -> 1.11 us
    unnamed x104 -> x86, local copies, waits for them, and re-layouts: 8.23 us -> 4.33 us
    ppermute x10 -> x7, starting transfers between devices: 13 us -> 9.37 us  [swap(): return lax.ppermute(values, 'group', [(0, 1), (1, 0)])]
  transfers between devices with their start and end apart: 12 -> 9, of which waited for: 5 -> 5; matrix products, arithmetic and copies ran while one was open for 11% -> 9% of each run, Pallas kernels for 0% -> 0%
where the time goes in v2:
time: 322 us
  Pallas kernels  203 us (63%)
  matrix products  39.3 us (12%)
  other arithmetic  31.1 us (10%)
  waiting for transfers between devices  20.8 us (6%)
  local copies, waits for them, and re-layouts  15.9 us (5%)
  starting transfers between devices  9.88 us (3%)
    pallas_call x1, Pallas kernels, replica_sum(): pl.pallas_call(functools.partial(sum_kernel, copies, tuple(pieces), swapp...  203 us
    ppermute x7, waiting for transfers between devices, swap(): return lax.ppermute(values, 'group', [(0, 1), (1, 0)])  19.9 us
    dot_general x5, matrix products, outer_sum(): lax.dot_general(left, right, (((0,), (0,)), ((), ())), preferred_element_...  16.6 us
    convert_element_type x6, other arithmetic, on_device(): a.astype(jnp.float32)  15.9 us
    dot_general x5, matrix products, times_transposed(): lax.dot_general(left, right, (((1,), (1,)), ((), ())), preferred_element_...  11.4 us
    ppermute x7, starting transfers between devices, swap(): return lax.ppermute(values, 'group', [(0, 1), (1, 0)])  9.37 us
  transfers between devices with their start and end apart: 9, of which 5 were waited for; matrix products, arithmetic and copies ran while one was open for 9% of the time, Pallas kernels for 0%

profile of v2, /device:TPU:0, one launch (start us, length us, event | category | flops | bytes accessed | tf_op | source)
XLA Modules:
  0.0 321.8 jit_solution(10045233659896589387)
XLA Ops:
  0.7 1.2 constant_dynamic-slice_fusion.1
  1.9 3.0 collective-permute-start.1
  4.9 2.1 concatenate.91
  7.0 1.0 constant_dynamic-slice_fusion
  8.1 2.1 collective-permute-start.3
  10.2 1.0 select_reduce_fusion
  11.1 1.5 select_compare_fusion
  12.9 0.6 multiply_multiply_fusion
  13.8 3.8 %collective-permute-done = bf16[1472]{0:T(1024)(128)(2,1)S(1)} collective-permute-done((bf16[1472]{0:T(1024)(128)(2,1)S(1)}, bf16[1472]{0:T(1024)(128)(2,1)S(1)}, u32[]{:S(2)}, u32[]{:S(2)}) %collective-permute-start) | collective-permute-done | bytes 2976 | tf_op jit(solution)/shard_map/ppermute | solution.py:252
  17.6 7.8 %collective-permute-done.3 = bf16[224,896]{1,0:T(8,128)(2,1)S(1)} collective-permute-done((bf16[224,896]{1,0:T(8,128)(2,1)S(1)}, bf16[224,896]{1,0:T(8,128)(2,1)S(1)}, u32[]{:S(2)}, u32[]{:S(2)}) %collective-permute-start.3) | collective-permute-done | bytes 401440 | tf_op jit(solution)/shard_map/ppermute | solution.py:252
  25.7 0.5 collective-permute-start.2
  26.2 0.8 collective-permute-done.4
  27.2 1.5 broadcast_select_fusion.3
  28.7 0.4 broadcast_select_fusion.1
  29.2 0.6 convolution_add_fusion
  30.5 0.8 copy-done.14
  31.7 0.6 subtract_convert_fusion
  32.3 0.5 copy.91
  32.7 0.5 copy.92
  33.4 0.5 fusion.61
  34.5 0.5 convolution_convert_fusion.5
  35.0 0.6 copy-done.8
  35.9 0.6 multiply_reduce_fusion.2
  36.7 1.8 collective-permute-start.5
  38.8 7.0 %collective-permute-done.5 = bf16[144,896]{1,0:T(8,128)(2,1)S(1)} collective-permute-done((bf16[144,896]{1,0:T(8,128)(2,1)S(1)}, bf16[144,896]{1,0:T(8,128)(2,1)S(1)}, u32[]{:S(2)}, u32[]{:S(2)}) %collective-permute-start.5) | collective-permute-done | bytes 258080 | tf_op jit(solution)/shard_map/ppermute | solution.py:252
  45.8 1.7 fusion.53
  47.5 1.7 fusion.54
  49.2 1.3 collective-permute-done.7
  50.5 3.5 %multiply_convert_fusion = (bf16[288,2432]{1,0:T(8,128)(2,1)S(1)}, bf16[288,2432]{1,0:T(8,128)(2,1)S(1)}, bf16[288,2432]{1,0:T(8,128)(2,1)S(1)}) fusion(f32[288,2432]{1,0:T(8,128)S(1)} %fusion.54, f32[288,2432]{1,0:T(8,128)S(1)} %fusion.53, bf16[2432,896]{1,0:T(8,128)(2,1)S(1)} %bitcast.169, bf16[144,896]{1,0:T(8,128)(2,1)S(1)} %collective-permute-done.7, ...), kind=kOutput, calls=%fused_computation.11 | convolution fusion | flops 1266683904 | bytes 14680064 | tf_op jit(solution)/shard_map/dot_general | solution.py:76
  54.1 1.7 fusion.63
  55.8 1.7 convolution_add_fusion.1
  57.5 1.8 collective-permute-start.8
  59.3 1.7 fusion.62
  61.0 0.4 collective-permute-start.6
  61.4 4.6 %convolution_convert_fusion.1 = bf16[896,2432]{1,0:T(8,128)(2,1)} fusion(bf16[288,2432]{1,0:T(8,128)(2,1)S(1)} %get-tuple-element.22, bf16[144,896]{1,0:T(8,128)(2,1)S(1)} %collective-permute-done.5, bf16[144,896]{1,0:T(8,128)(2,1)S(1)} %multiply_convert_fusion.3), kind=kOutput, calls=%fused_computation.3 | convolution fusion | flops 1258356736 | bytes 6275072 | tf_op jit(solution)/shard_map/dot_general | solution.py:70
  66.0 4.6 %convolution_convert_fusion.2 = bf16[896,2432]{1,0:T(8,128)(2,1)} fusion(bf16[288,2432]{1,0:T(8,128)(2,1)S(1)} %get-tuple-element.23, bf16[144,896]{1,0:T(8,128)(2,1)S(1)} %collective-permute-done.5, bf16[144,896]{1,0:T(8,128)(2,1)S(1)} %multiply_convert_fusion.3), kind=kOutput, calls=%fused_computation.4 | convolution fusion | flops 1258356736 | bytes 6275072 | tf_op jit(solution)/shard_map/dot_general | solution.py:70
  70.6 4.7 %convolution_convert_fusion = bf16[2432,896]{1,0:T(8,128)(2,1)} fusion(bf16[288,2432]{1,0:T(8,128)(2,1)S(1)} %get-tuple-element.24, bf16[144,896]{1,0:T(8,128)(2,1)S(1)} %collective-permute-done.7, bf16[144,896]{1,0:T(8,128)(2,1)S(1)} %bitcast.161), kind=kOutput, calls=%fused_computation.2 | convolution fusion | flops 1258356736 | bytes 6275072 | tf_op jit(solution)/shard_map/dot_general | solution.py:70
  75.3 0.8 multiply_reduce_fusion
  76.1 1.1 subtract_add_fusion
  77.1 1.3 convolution_convert_fusion.6
  78.4 1.1 copy.125
  79.6 1.6 fusion.3
  81.2 0.5 fusion.10
  82.3 1.1 convolution_bitcast_fusion
  83.4 1.1 fusion.27
  84.5 1.8 convolution_convert_fusion.4
  86.4 0.6 copy.126
  87.0 0.6 copy.127
  88.0 0.4 pad_maximum_fusion.5
  88.4 0.3 reshape.520
  89.4 0.9 convolution_convert_fusion.3
  90.3 3.1 fusion.21
  93.9 1.9 fusion.56
  96.1 2.2 fusion.1
  98.3 203.4 %replica_sum.1 = (bf16[16,56,2432]{2,1,0:T(8,128)(2,1)}, bf16[16,56,2432]{2,1,0:T(8,128)(2,1)}, bf16[16,152,896]{2,1,0:T(8,128)(2,1)}, bf16[16,64,1024]{2,1,0:T(8,128)(2,1)}) custom-call(bf16[16,56,2432]{2,1,0:T(8,128)(2,1)} %bitcast.144, bf16[16,56,2432]{2,1,0:T(8,128)(2,1)} %bitcast.143, bf16[16,152,896]{2,1,0:T(8,128)(2,1)} %bitcast.145, ...), custom_call_target="tpu_custom_call" | custom-call | tf_op jit(solution)/shard_map/replica_sum/pallas_call | solution.py:230
  301.8 1.9 fusion.55
  303.6 1.3 slice_convert_fusion
  304.9 1.4 fusion.11
  306.3 0.7 fusion.58
  307.0 0.6 slice_reduce_fusion
  307.6 4.4 %bitcast_convert_fusion = f32[2432,896]{1,0:T(8,128)} fusion(bf16[16,152,896]{2,1,0:T(8,128)(2,1)S(1)} %bitcast.142), kind=kLoop, calls=%fused_computation.5 | loop fusion | flops 2179072 | bytes 13074432 | tf_op jit(solution)/shard_map/convert_element_type | solution.py:470
  312.0 4.4 %bitcast_convert_fusion.1 = f32[896,2432]{1,0:T(8,128)} fusion(bf16[16,56,2432]{2,1,0:T(8,128)(2,1)S(1)} %bitcast.140), kind=kLoop, calls=%fused_computation.6 | loop fusion | flops 2179072 | bytes 13074432 | tf_op jit(solution)/shard_map/convert_element_type | solution.py:470
  316.4 4.4 %bitcast_convert_fusion.2 = f32[896,2432]{1,0:T(8,128)} fusion(bf16[16,56,2432]{2,1,0:T(8,128)(2,1)S(1)} %bitcast.138), kind=kLoop, calls=%fused_computation.7 | loop fusion | flops 2179072 | bytes 13074432 | tf_op jit(solution)/shard_map/convert_element_type | solution.py:470
  320.8 1.0 fusion.18
  (143 shorter events, 6.0 us)
Async XLA Ops:
  0.6 11.9 %copy-start.1 = (bf16[1,144,896]{2,1,0:T(8,128)(2,1)S(1)}, bf16[1,144,896]{2,1,0:T(8,128)(2,1)}, u32[]{:S(2)}) copy-start(bf16[1,144,896]{2,1,0:T(8,128)(2,1)} %param.11) | copy-start | bytes 774148
  0.7 26.5 %copy-start.5 = (bf16[448,896]{1,0:T(8,128)(2,1)S(1)}, bf16[448,896]{1,0:T(8,128)(2,1)}, u32[]{:S(2)}) copy-start(bf16[448,896]{1,0:T(8,128)(2,1)} %param.16) | copy-start | bytes 2408452
  1.9 23.9 %collective-permute-start.1 = (bf16[224,1152]{1,0:T(8,128)(2,1)S(1)}, bf16[224,1152]{1,0:T(8,128)(2,1)S(1)}, u32[]{:S(2)}, u32[]{:S(2)}) collective-permute-start(bf16[224,1152]{1,0:T(8,128)(2,1)S(1)} %constant_dynamic-slice_fusion.1), channel_id=1, source_target_pairs={{0,16},{16,0},{1,17},{17,1},{2,18},{18,2},{3,19},{19,3},{4,20},{20... | collective-permute-start | bytes 1548296 | tf_op jit(solution)/shard_map/ppermute | solution.py:252
  7.0 10.5 %collective-permute-start = (bf16[1472]{0:T(1024)(128)(2,1)S(1)}, bf16[1472]{0:T(1024)(128)(2,1)S(1)}, u32[]{:S(2)}, u32[]{:S(2)}) collective-permute-start(bf16[1472]{0:T(1024)(128)(2,1)S(1)} %concatenate.91), channel_id=1, source_target_pairs={{0,16},{16,0},{1,17},{17,1},{2,18},{18,2},{3,19},{19,3},{4,20},{20... | collective-permute-start | bytes 8840 | tf_op jit(solution)/shard_map/ppermute | solution.py:252
  8.1 17.2 %collective-permute-start.3 = (bf16[224,896]{1,0:T(8,128)(2,1)S(1)}, bf16[224,896]{1,0:T(8,128)(2,1)S(1)}, u32[]{:S(2)}, u32[]{:S(2)}) collective-permute-start(bf16[224,896]{1,0:T(8,128)(2,1)S(1)} %constant_dynamic-slice_fusion), channel_id=1, source_target_pairs={{0,16},{16,0},{1,17},{17,1},{2,18},{18,2},{3,19},{19,3},{4,20},{20... | collective-permute-start | bytes 1204232 | tf_op jit(solution)/shard_map/ppermute | solution.py:252
  12.9 20.4 %copy-start.17 = (f32[144,32]{0,1:T(8,128)}, f32[144,32]{0,1:T(8,128)S(1)}, u32[]{:S(2)}) copy-start(f32[144,32]{0,1:T(8,128)S(1)} %get-tuple-element.58) | copy-start | bytes 55300
  13.5 15.6 %copy-start.27 = (f32[144]{0:T(256)}, f32[144]{0:T(256)S(1)}, u32[]{:S(2)}) copy-start(f32[144]{0:T(256)S(1)} %get-tuple-element.60) | copy-start | bytes 1732
  13.6 18.0 %copy-start.10 = (f32[144,32]{1,0:T(8,128)}, f32[144,32]{1,0:T(8,128)S(1)}, u32[]{:S(2)}) copy-start(f32[144,32]{1,0:T(8,128)S(1)} %copy.89) | copy-start | bytes 55300
  13.7 17.9 %copy-start.12 = (f32[144,32]{1,0:T(8,128)}, f32[144,32]{1,0:T(8,128)S(1)}, u32[]{:S(2)}) copy-start(f32[144,32]{1,0:T(8,128)S(1)} %copy.90) | copy-start | bytes 55300
  25.3 1.7 collective-permute-start.4
  25.7 2.9 collective-permute-start.2
  27.2 1.6 copy-start
  29.1 1.0 copy-start.6
  29.2 1.3 copy-start.7
  30.4 0.8 copy-start.14
  31.6 1.6 slice-start.6
  32.2 1.1 copy-start.26
  33.3 0.9 copy-start.22
  33.4 0.9 copy-start.24
  34.5 2.0 copy-start.15
  34.5 1.2 copy-start.8
  34.5 1.4 copy-start.9
  35.0 1.7 copy-start.3
  35.9 2.6 copy-start.21
  35.9 9.9 %copy-start.31 = (bf16[896,2432]{1,0:T(8,128)(2,1)S(1)}, bf16[896,2432]{1,0:T(8,128)(2,1)}, u32[]{:S(2)}) copy-start(bf16[896,2432]{1,0:T(8,128)(2,1)} %param.19) | copy-start | bytes 13074436
  36.7 9.1 %collective-permute-start.5 = (bf16[144,896]{1,0:T(8,128)(2,1)S(1)}, bf16[144,896]{1,0:T(8,128)(2,1)S(1)}, u32[]{:S(2)}, u32[]{:S(2)}) collective-permute-start(bf16[144,896]{1,0:T(8,128)(2,1)S(1)} %multiply_convert_fusion.3), channel_id=1, source_target_pairs={{0,16},{16,0},{1,17},{17,1},{2,18},{18,2},{3,19},{19,3},{4,20},{20... | collective-permute-start | bytes 774152 | tf_op jit(solution)/shard_map/ppermute | solution.py:252
  38.5 9.0 %slice-start.7 = ((s8[4358144]{0:T(1024)(128)(4,1)}), s8[4194304]{0:T(1024)(128)(4,1)S(1)}, s32[]{:S(2)}) async-start(s8[4358144]{0:T(1024)(128)(4,1)} %bitcast.166), calls=%async_computation.7 | async-start | bytes 8388608
  38.5 9.0 %slice-start.8 = ((s8[4358144]{0:T(1024)(128)(4,1)}), s8[163840]{0:T(1024)(128)(4,1)S(1)}, s32[]{:S(2)}) async-start(s8[4358144]{0:T(1024)(128)(4,1)} %bitcast.166), calls=%async_computation.8 | async-start | bytes 327680
  38.5 12.0 %collective-permute-start.7 = (bf16[144,896]{1,0:T(8,128)(2,1)S(1)}, bf16[144,896]{1,0:T(8,128)(2,1)S(1)}, u32[]{:S(2)}, u32[]{:S(2)}) collective-permute-start(bf16[144,896]{1,0:T(8,128)(2,1)S(1)} %bitcast.159), channel_id=1, source_target_pairs={{0,16},{16,0},{1,17},{17,1},{2,18},{18,2},{3,19},{19,3},{4,20},{20... | collective-permute-start | bytes 774152 | tf_op jit(solution)/shard_map/ppermute | solution.py:252
  45.8 4.7 %slice-start.9 = ((s8[4358144]{0:T(1024)(128)(4,1)}), s8[4194304]{0:T(1024)(128)(4,1)S(1)}, s32[]{:S(2)}) async-start(s8[4358144]{0:T(1024)(128)(4,1)} %bitcast.168), calls=%async_computation.9 | async-start | bytes 8388608
  47.5 3.0 slice-start.10
  57.5 17.8 %collective-permute-start.8 = (bf16[144,896]{1,0:T(8,128)(2,1)S(1)}, bf16[144,896]{1,0:T(8,128)(2,1)S(1)}, u32[]{:S(2)}, u32[]{:S(2)}) collective-permute-start(bf16[144,896]{1,0:T(8,128)(2,1)S(1)} %slice.205), channel_id=1, source_target_pairs={{0,16},{16,0},{1,17},{17,1},{2,18},{18,2},{3,19},{19,3},{4,20},{20... | collective-permute-start | bytes 774152 | tf_op jit(solution)/shard_map/ppermute | solution.py:252
  61.0 15.0 %collective-permute-start.6 = (bf16[144,896]{1,0:T(8,128)(2,1)S(1)}, bf16[144,896]{1,0:T(8,128)(2,1)S(1)}, u32[]{:S(2)}, u32[]{:S(2)}) collective-permute-start(bf16[144,896]{1,0:T(8,128)(2,1)S(1)} %slice.206), channel_id=1, source_target_pairs={{0,16},{16,0},{1,17},{17,1},{2,18},{18,2},{3,19},{19,3},{4,20},{20... | collective-permute-start | bytes 774152 | tf_op jit(solution)/shard_map/ppermute | solution.py:252
  81.2 0.8 copy-start.23
  81.2 0.8 copy-start.25
  82.3 2.3 copy-start.4
  86.4 1.2 copy-start.11
  86.4 1.2 copy-start.13
  87.9 0.9 copy-start.16
  87.9 0.9 copy-start.18
  88.3 0.9 copy-start.19
  88.3 1.0 copy-start.2
  88.4 1.0 copy-start.28
  90.3 3.3 %copy-start.29 = (bf16[896]{0:T(1024)(128)(2,1)S(1)}, bf16[896]{0:T(1024)(128)(2,1)}, u32[]{:S(2)}) copy-start(bf16[896]{0:T(1024)(128)(2,1)} %get-tuple-element.18) | copy-start | bytes 5380
  301.7 5.9 %slice-start.4 = ((s8[4358144]{0:T(1024)(128)(4,1)}), s8[4194304]{0:T(1024)(128)(4,1)S(1)}, s32[]{:S(2)}) async-start(s8[4358144]{0:T(1024)(128)(4,1)} %bitcast.141), calls=%async_computation.4 | async-start | bytes 8388608
  303.6 4.0 %slice-start.5 = ((s8[4358144]{0:T(1024)(128)(4,1)}), s8[163840]{0:T(1024)(128)(4,1)S(1)}, s32[]{:S(2)}) async-start(s8[4358144]{0:T(1024)(128)(4,1)} %bitcast.141), calls=%async_computation.5 | async-start | bytes 327680
  306.3 5.7 %slice-start.2 = ((s8[4358144]{0:T(1024)(128)(4,1)}), s8[4194304]{0:T(1024)(128)(4,1)S(1)}, s32[]{:S(2)}) async-start(s8[4358144]{0:T(1024)(128)(4,1)} %bitcast.139), calls=%async_computation.2 | async-start | bytes 8388608
  307.6 4.4 %slice-start.3 = ((s8[4358144]{0:T(1024)(128)(4,1)}), s8[163840]{0:T(1024)(128)(4,1)S(1)}, s32[]{:S(2)}) async-start(s8[4358144]{0:T(1024)(128)(4,1)} %bitcast.139), calls=%async_computation.3 | async-start | bytes 327680
  307.6 8.8 %slice-start = ((s8[4358144]{0:T(1024)(128)(4,1)}), s8[4194304]{0:T(1024)(128)(4,1)S(1)}, s32[]{:S(2)}) async-start(s8[4358144]{0:T(1024)(128)(4,1)} %bitcast.137), calls=%async_computation | async-start | bytes 8388608
  312.0 4.4 %slice-start.1 = ((s8[4358144]{0:T(1024)(128)(4,1)}), s8[163840]{0:T(1024)(128)(4,1)S(1)}, s32[]{:S(2)}) async-start(s8[4358144]{0:T(1024)(128)(4,1)} %bitcast.137), calls=%async_computation.1 | async-start | bytes 327680
  316.4 4.4 %copy-start.20 = (f32[144,896]{1,0:T(8,128)S(1)}, f32[144,896]{1,0:T(8,128)}, u32[]{:S(2)}) copy-start(f32[144,896]{1,0:T(8,128)} %get-tuple-element.69) | copy-start | bytes 1548292
  316.4 4.4 %copy-start.30 = (f32[144]{0:T(256)S(1)}, f32[144]{0:T(256)}, u32[]{:S(2)}) copy-start(f32[144]{0:T(256)} %get-tuple-element.59) | copy-start | bytes 1732

commit v3 on v2

--- a/solution.py
+++ b/solution.py
@@ -220,7 +220,7 @@
     pieces = []
     for which, array in enumerate(arrays):
         columns = array.shape[-1]
-        cut = columns // 256 * 128
+        cut = columns * 4 // 640 * 128
         pieces += [(which, 0, cut, False, which), (which, cut, columns - cut, True, which)]
     stages = copies.bit_length() - 1
     n, count = len(pieces), len(arrays)

time: 322 us -> 312 us (0.969)
  Pallas kernels: 203 us -> 193 us
    pallas_call x1, Pallas kernels: 203 us -> 193 us  [replica_sum(): pl.pallas_call(functools.partial(sum_kernel, copies, tuple(pieces), swapp...]
where the time goes in v3:
time: 312 us; the launch traced here: 311 us
  Pallas kernels  193 us (62%)
  matrix products  39.3 us (13%)
  other arithmetic  31.1 us (10%)
  waiting for transfers between devices  20.8 us (7%)
  local copies, waits for them, and re-layouts  15.9 us (5%)
  starting transfers between devices  9.88 us (3%)
    pallas_call x1, Pallas kernels, replica_sum(): pl.pallas_call(functools.partial(sum_kernel, copies, tuple(pieces), swapp...  193 us
    ppermute x7, waiting for transfers between devices, swap(): return lax.ppermute(values, 'group', [(0, 1), (1, 0)])  19.9 us
    dot_general x5, matrix products, outer_sum(): lax.dot_general(left, right, (((0,), (0,)), ((), ())), preferred_element_...  16.6 us
    convert_element_type x6, other arithmetic, on_device(): a.astype(jnp.float32)  15.9 us
    dot_general x5, matrix products, times_transposed(): lax.dot_general(left, right, (((1,), (1,)), ((), ())), preferred_element_...  11.4 us
    ppermute x7, starting transfers between devices, swap(): return lax.ppermute(values, 'group', [(0, 1), (1, 0)])  9.37 us
  transfers between devices with their start and end apart: 9, of which 5 were waited for; matrix products, arithmetic and copies ran while one was open for 9% of the time, Pallas kernels for 0%

profile of v3, /device:TPU:0, one launch (start us, length us, event | category | flops | bytes accessed | tf_op | source)
XLA Modules:
  0.0 311.4 jit_solution(11573574878293089831)
XLA Ops:
  0.7 1.2 constant_dynamic-slice_fusion.1
  1.9 3.0 collective-permute-start.1
  4.9 2.1 concatenate.91
  7.0 1.0 constant_dynamic-slice_fusion
  8.1 2.1 collective-permute-start.3
  10.2 1.0 select_reduce_fusion
  11.1 1.5 select_compare_fusion
  12.9 0.6 multiply_multiply_fusion
  13.8 3.8 %collective-permute-done = bf16[1472]{0:T(1024)(128)(2,1)S(1)} collective-permute-done((bf16[1472]{0:T(1024)(128)(2,1)S(1)}, bf16[1472]{0:T(1024)(128)(2,1)S(1)}, u32[]{:S(2)}, u32[]{:S(2)}) %collective-permute-start) | collective-permute-done | bytes 2976 | tf_op jit(solution)/shard_map/ppermute | solution.py:252
  17.6 7.8 %collective-permute-done.3 = bf16[224,896]{1,0:T(8,128)(2,1)S(1)} collective-permute-done((bf16[224,896]{1,0:T(8,128)(2,1)S(1)}, bf16[224,896]{1,0:T(8,128)(2,1)S(1)}, u32[]{:S(2)}, u32[]{:S(2)}) %collective-permute-start.3) | collective-permute-done | bytes 401440 | tf_op jit(solution)/shard_map/ppermute | solution.py:252
  25.7 0.5 collective-permute-start.2
  26.2 0.8 collective-permute-done.4
  27.2 1.5 broadcast_select_fusion.3
  28.7 0.4 broadcast_select_fusion.1
  29.2 0.6 convolution_add_fusion
  30.5 0.8 copy-done.14
  31.7 0.6 subtract_convert_fusion
  32.3 0.5 copy.91
  32.7 0.5 copy.92
  33.4 0.5 fusion.61
  34.5 0.5 convolution_convert_fusion.5
  35.0 0.6 copy-done.8
  35.9 0.6 multiply_reduce_fusion.2
  36.7 1.8 collective-permute-start.5
  38.8 7.0 %collective-permute-done.5 = bf16[144,896]{1,0:T(8,128)(2,1)S(1)} collective-permute-done((bf16[144,896]{1,0:T(8,128)(2,1)S(1)}, bf16[144,896]{1,0:T(8,128)(2,1)S(1)}, u32[]{:S(2)}, u32[]{:S(2)}) %collective-permute-start.5) | collective-permute-done | bytes 258080 | tf_op jit(solution)/shard_map/ppermute | solution.py:252
  45.8 1.7 fusion.53
  47.5 1.7 fusion.54
  49.2 1.3 collective-permute-done.7
  50.5 3.5 %multiply_convert_fusion = (bf16[288,2432]{1,0:T(8,128)(2,1)S(1)}, bf16[288,2432]{1,0:T(8,128)(2,1)S(1)}, bf16[288,2432]{1,0:T(8,128)(2,1)S(1)}) fusion(f32[288,2432]{1,0:T(8,128)S(1)} %fusion.54, f32[288,2432]{1,0:T(8,128)S(1)} %fusion.53, bf16[2432,896]{1,0:T(8,128)(2,1)S(1)} %bitcast.169, bf16[144,896]{1,0:T(8,128)(2,1)S(1)} %collective-permute-done.7, ...), kind=kOutput, calls=%fused_computation.11 | convolution fusion | flops 1266683904 | bytes 14680064 | tf_op jit(solution)/shard_map/dot_general | solution.py:76
  54.1 1.7 fusion.63
  55.8 1.7 convolution_add_fusion.1
  57.5 1.8 collective-permute-start.8
  59.3 1.7 fusion.62
  61.0 0.4 collective-permute-start.6
  61.4 4.6 %convolution_convert_fusion.1 = bf16[896,2432]{1,0:T(8,128)(2,1)} fusion(bf16[288,2432]{1,0:T(8,128)(2,1)S(1)} %get-tuple-element.22, bf16[144,896]{1,0:T(8,128)(2,1)S(1)} %collective-permute-done.5, bf16[144,896]{1,0:T(8,128)(2,1)S(1)} %multiply_convert_fusion.3), kind=kOutput, calls=%fused_computation.3 | convolution fusion | flops 1258356736 | bytes 6275072 | tf_op jit(solution)/shard_map/dot_general | solution.py:70
  66.0 4.6 %convolution_convert_fusion.2 = bf16[896,2432]{1,0:T(8,128)(2,1)} fusion(bf16[288,2432]{1,0:T(8,128)(2,1)S(1)} %get-tuple-element.23, bf16[144,896]{1,0:T(8,128)(2,1)S(1)} %collective-permute-done.5, bf16[144,896]{1,0:T(8,128)(2,1)S(1)} %multiply_convert_fusion.3), kind=kOutput, calls=%fused_computation.4 | convolution fusion | flops 1258356736 | bytes 6275072 | tf_op jit(solution)/shard_map/dot_general | solution.py:70
  70.6 4.7 %convolution_convert_fusion = bf16[2432,896]{1,0:T(8,128)(2,1)} fusion(bf16[288,2432]{1,0:T(8,128)(2,1)S(1)} %get-tuple-element.24, bf16[144,896]{1,0:T(8,128)(2,1)S(1)} %collective-permute-done.7, bf16[144,896]{1,0:T(8,128)(2,1)S(1)} %bitcast.161), kind=kOutput, calls=%fused_computation.2 | convolution fusion | flops 1258356736 | bytes 6275072 | tf_op jit(solution)/shard_map/dot_general | solution.py:70
  75.3 0.8 multiply_reduce_fusion
  76.1 1.1 subtract_add_fusion
  77.1 1.3 convolution_convert_fusion.6
  78.4 1.1 copy.125
  79.6 1.6 fusion.3
  81.2 0.5 fusion.10
  82.3 1.1 convolution_bitcast_fusion
  83.4 1.1 fusion.27
  84.5 1.8 convolution_convert_fusion.4
  86.4 0.6 copy.126
  87.0 0.6 copy.127
  88.0 0.4 pad_maximum_fusion.5
  88.4 0.3 reshape.520
  89.4 0.9 convolution_convert_fusion.3
  90.3 3.1 fusion.21
  93.9 1.9 fusion.56
  96.1 2.2 fusion.1
  98.3 193.0 %replica_sum.1 = (bf16[16,56,2432]{2,1,0:T(8,128)(2,1)}, bf16[16,56,2432]{2,1,0:T(8,128)(2,1)}, bf16[16,152,896]{2,1,0:T(8,128)(2,1)}, bf16[16,64,1024]{2,1,0:T(8,128)(2,1)}) custom-call(bf16[16,56,2432]{2,1,0:T(8,128)(2,1)} %bitcast.144, bf16[16,56,2432]{2,1,0:T(8,128)(2,1)} %bitcast.143, bf16[16,152,896]{2,1,0:T(8,128)(2,1)} %bitcast.145, ...), custom_call_target="tpu_custom_call" | custom-call | tf_op jit(solution)/shard_map/replica_sum/pallas_call | solution.py:230
  291.3 1.9 fusion.55
  293.2 1.3 slice_convert_fusion
  294.4 1.4 fusion.11
  295.9 0.7 fusion.58
  296.5 0.6 slice_reduce_fusion
  297.2 4.4 %bitcast_convert_fusion = f32[2432,896]{1,0:T(8,128)} fusion(bf16[16,152,896]{2,1,0:T(8,128)(2,1)S(1)} %bitcast.142), kind=kLoop, calls=%fused_computation.5 | loop fusion | flops 2179072 | bytes 13074432 | tf_op jit(solution)/shard_map/convert_element_type | solution.py:470
  301.6 4.4 %bitcast_convert_fusion.1 = f32[896,2432]{1,0:T(8,128)} fusion(bf16[16,56,2432]{2,1,0:T(8,128)(2,1)S(1)} %bitcast.140), kind=kLoop, calls=%fused_computation.6 | loop fusion | flops 2179072 | bytes 13074432 | tf_op jit(solution)/shard_map/convert_element_type | solution.py:470
  306.0 4.4 %bitcast_convert_fusion.2 = f32[896,2432]{1,0:T(8,128)} fusion(bf16[16,56,2432]{2,1,0:T(8,128)(2,1)S(1)} %bitcast.138), kind=kLoop, calls=%fused_computation.7 | loop fusion | flops 2179072 | bytes 13074432 | tf_op jit(solution)/shard_map/convert_element_type | solution.py:470
  310.4 1.0 fusion.18
  (143 shorter events, 6.0 us)
Async XLA Ops:
  0.6 11.9 %copy-start.1 = (bf16[1,144,896]{2,1,0:T(8,128)(2,1)S(1)}, bf16[1,144,896]{2,1,0:T(8,128)(2,1)}, u32[]{:S(2)}) copy-start(bf16[1,144,896]{2,1,0:T(8,128)(2,1)} %param.11) | copy-start | bytes 774148
  0.7 26.5 %copy-start.5 = (bf16[448,896]{1,0:T(8,128)(2,1)S(1)}, bf16[448,896]{1,0:T(8,128)(2,1)}, u32[]{:S(2)}) copy-start(bf16[448,896]{1,0:T(8,128)(2,1)} %param.16) | copy-start | bytes 2408452
  1.9 23.9 %collective-permute-start.1 = (bf16[224,1152]{1,0:T(8,128)(2,1)S(1)}, bf16[224,1152]{1,0:T(8,128)(2,1)S(1)}, u32[]{:S(2)}, u32[]{:S(2)}) collective-permute-start(bf16[224,1152]{1,0:T(8,128)(2,1)S(1)} %constant_dynamic-slice_fusion.1), channel_id=1, source_target_pairs={{0,16},{16,0},{1,17},{17,1},{2,18},{18,2},{3,19},{19,3},{4,20},{20... | collective-permute-start | bytes 1548296 | tf_op jit(solution)/shard_map/ppermute | solution.py:252
  7.0 10.5 %collective-permute-start = (bf16[1472]{0:T(1024)(128)(2,1)S(1)}, bf16[1472]{0:T(1024)(128)(2,1)S(1)}, u32[]{:S(2)}, u32[]{:S(2)}) collective-permute-start(bf16[1472]{0:T(1024)(128)(2,1)S(1)} %concatenate.91), channel_id=1, source_target_pairs={{0,16},{16,0},{1,17},{17,1},{2,18},{18,2},{3,19},{19,3},{4,20},{20... | collective-permute-start | bytes 8840 | tf_op jit(solution)/shard_map/ppermute | solution.py:252
  8.1 17.2 %collective-permute-start.3 = (bf16[224,896]{1,0:T(8,128)(2,1)S(1)}, bf16[224,896]{1,0:T(8,128)(2,1)S(1)}, u32[]{:S(2)}, u32[]{:S(2)}) collective-permute-start(bf16[224,896]{1,0:T(8,128)(2,1)S(1)} %constant_dynamic-slice_fusion), channel_id=1, source_target_pairs={{0,16},{16,0},{1,17},{17,1},{2,18},{18,2},{3,19},{19,3},{4,20},{20... | collective-permute-start | bytes 1204232 | tf_op jit(solution)/shard_map/ppermute | solution.py:252
  12.9 20.4 %copy-start.17 = (f32[144,32]{0,1:T(8,128)}, f32[144,32]{0,1:T(8,128)S(1)}, u32[]{:S(2)}) copy-start(f32[144,32]{0,1:T(8,128)S(1)} %get-tuple-element.58) | copy-start | bytes 55300
  13.5 15.6 %copy-start.27 = (f32[144]{0:T(256)}, f32[144]{0:T(256)S(1)}, u32[]{:S(2)}) copy-start(f32[144]{0:T(256)S(1)} %get-tuple-element.60) | copy-start | bytes 1732
  13.6 18.0 %copy-start.10 = (f32[144,32]{1,0:T(8,128)}, f32[144,32]{1,0:T(8,128)S(1)}, u32[]{:S(2)}) copy-start(f32[144,32]{1,0:T(8,128)S(1)} %copy.89) | copy-start | bytes 55300
  13.7 17.9 %copy-start.12 = (f32[144,32]{1,0:T(8,128)}, f32[144,32]{1,0:T(8,128)S(1)}, u32[]{:S(2)}) copy-start(f32[144,32]{1,0:T(8,128)S(1)} %copy.90) | copy-start | bytes 55300
  25.3 1.7 collective-permute-start.4
  25.7 2.9 collective-permute-start.2
  27.2 1.6 copy-start
  29.1 1.0 copy-start.6
  29.2 1.3 copy-start.7
  30.4 0.8 copy-start.14
  31.6 1.6 slice-start.6
  32.2 1.1 copy-start.26
  33.3 0.9 copy-start.22
  33.4 0.9 copy-start.24
  34.5 2.0 copy-start.15
  34.5 1.2 copy-start.8
  34.5 1.4 copy-start.9
  35.0 1.7 copy-start.3
  35.9 2.6 copy-start.21
  35.9 9.9 %copy-start.31 = (bf16[896,2432]{1,0:T(8,128)(2,1)S(1)}, bf16[896,2432]{1,0:T(8,128)(2,1)}, u32[]{:S(2)}) copy-start(bf16[896,2432]{1,0:T(8,128)(2,1)} %param.19) | copy-start | bytes 13074436
  36.7 9.1 %collective-permute-start.5 = (bf16[144,896]{1,0:T(8,128)(2,1)S(1)}, bf16[144,896]{1,0:T(8,128)(2,1)S(1)}, u32[]{:S(2)}, u32[]{:S(2)}) collective-permute-start(bf16[144,896]{1,0:T(8,128)(2,1)S(1)} %multiply_convert_fusion.3), channel_id=1, source_target_pairs={{0,16},{16,0},{1,17},{17,1},{2,18},{18,2},{3,19},{19,3},{4,20},{20... | collective-permute-start | bytes 774152 | tf_op jit(solution)/shard_map/ppermute | solution.py:252
  38.5 9.0 %slice-start.7 = ((s8[4358144]{0:T(1024)(128)(4,1)}), s8[4194304]{0:T(1024)(128)(4,1)S(1)}, s32[]{:S(2)}) async-start(s8[4358144]{0:T(1024)(128)(4,1)} %bitcast.166), calls=%async_computation.7 | async-start | bytes 8388608
  38.5 9.0 %slice-start.8 = ((s8[4358144]{0:T(1024)(128)(4,1)}), s8[163840]{0:T(1024)(128)(4,1)S(1)}, s32[]{:S(2)}) async-start(s8[4358144]{0:T(1024)(128)(4,1)} %bitcast.166), calls=%async_computation.8 | async-start | bytes 327680
  38.5 12.0 %collective-permute-start.7 = (bf16[144,896]{1,0:T(8,128)(2,1)S(1)}, bf16[144,896]{1,0:T(8,128)(2,1)S(1)}, u32[]{:S(2)}, u32[]{:S(2)}) collective-permute-start(bf16[144,896]{1,0:T(8,128)(2,1)S(1)} %bitcast.159), channel_id=1, source_target_pairs={{0,16},{16,0},{1,17},{17,1},{2,18},{18,2},{3,19},{19,3},{4,20},{20... | collective-permute-start | bytes 774152 | tf_op jit(solution)/shard_map/ppermute | solution.py:252
  45.8 4.7 %slice-start.9 = ((s8[4358144]{0:T(1024)(128)(4,1)}), s8[4194304]{0:T(1024)(128)(4,1)S(1)}, s32[]{:S(2)}) async-start(s8[4358144]{0:T(1024)(128)(4,1)} %bitcast.168), calls=%async_computation.9 | async-start | bytes 8388608
  47.5 3.0 slice-start.10
  57.5 17.8 %collective-permute-start.8 = (bf16[144,896]{1,0:T(8,128)(2,1)S(1)}, bf16[144,896]{1,0:T(8,128)(2,1)S(1)}, u32[]{:S(2)}, u32[]{:S(2)}) collective-permute-start(bf16[144,896]{1,0:T(8,128)(2,1)S(1)} %slice.205), channel_id=1, source_target_pairs={{0,16},{16,0},{1,17},{17,1},{2,18},{18,2},{3,19},{19,3},{4,20},{20... | collective-permute-start | bytes 774152 | tf_op jit(solution)/shard_map/ppermute | solution.py:252
  61.0 15.0 %collective-permute-start.6 = (bf16[144,896]{1,0:T(8,128)(2,1)S(1)}, bf16[144,896]{1,0:T(8,128)(2,1)S(1)}, u32[]{:S(2)}, u32[]{:S(2)}) collective-permute-start(bf16[144,896]{1,0:T(8,128)(2,1)S(1)} %slice.206), channel_id=1, source_target_pairs={{0,16},{16,0},{1,17},{17,1},{2,18},{18,2},{3,19},{19,3},{4,20},{20... | collective-permute-start | bytes 774152 | tf_op jit(solution)/shard_map/ppermute | solution.py:252
  81.2 0.8 copy-start.23
  81.2 0.8 copy-start.25
  82.3 2.3 copy-start.4
  86.4 1.2 copy-start.11
  86.4 1.2 copy-start.13
  87.9 0.9 copy-start.16
  87.9 0.9 copy-start.18
  88.3 0.9 copy-start.19
  88.3 1.0 copy-start.2
  88.4 1.0 copy-start.28
  90.3 3.3 %copy-start.29 = (bf16[896]{0:T(1024)(128)(2,1)S(1)}, bf16[896]{0:T(1024)(128)(2,1)}, u32[]{:S(2)}) copy-start(bf16[896]{0:T(1024)(128)(2,1)} %get-tuple-element.18) | copy-start | bytes 5380
  291.3 5.9 %slice-start.4 = ((s8[4358144]{0:T(1024)(128)(4,1)}), s8[4194304]{0:T(1024)(128)(4,1)S(1)}, s32[]{:S(2)}) async-start(s8[4358144]{0:T(1024)(128)(4,1)} %bitcast.141), calls=%async_computation.4 | async-start | bytes 8388608
  293.2 4.0 %slice-start.5 = ((s8[4358144]{0:T(1024)(128)(4,1)}), s8[163840]{0:T(1024)(128)(4,1)S(1)}, s32[]{:S(2)}) async-start(s8[4358144]{0:T(1024)(128)(4,1)} %bitcast.141), calls=%async_computation.5 | async-start | bytes 327680
  295.9 5.7 %slice-start.2 = ((s8[4358144]{0:T(1024)(128)(4,1)}), s8[4194304]{0:T(1024)(128)(4,1)S(1)}, s32[]{:S(2)}) async-start(s8[4358144]{0:T(1024)(128)(4,1)} %bitcast.139), calls=%async_computation.2 | async-start | bytes 8388608
  297.2 4.4 %slice-start.3 = ((s8[4358144]{0:T(1024)(128)(4,1)}), s8[163840]{0:T(1024)(128)(4,1)S(1)}, s32[]{:S(2)}) async-start(s8[4358144]{0:T(1024)(128)(4,1)} %bitcast.139), calls=%async_computation.3 | async-start | bytes 327680
  297.2 8.8 %slice-start = ((s8[4358144]{0:T(1024)(128)(4,1)}), s8[4194304]{0:T(1024)(128)(4,1)S(1)}, s32[]{:S(2)}) async-start(s8[4358144]{0:T(1024)(128)(4,1)} %bitcast.137), calls=%async_computation | async-start | bytes 8388608
  301.6 4.4 %slice-start.1 = ((s8[4358144]{0:T(1024)(128)(4,1)}), s8[163840]{0:T(1024)(128)(4,1)S(1)}, s32[]{:S(2)}) async-start(s8[4358144]{0:T(1024)(128)(4,1)} %bitcast.137), calls=%async_computation.1 | async-start | bytes 327680
  306.0 4.4 %copy-start.20 = (f32[144,896]{1,0:T(8,128)S(1)}, f32[144,896]{1,0:T(8,128)}, u32[]{:S(2)}) copy-start(f32[144,896]{1,0:T(8,128)} %get-tuple-element.69) | copy-start | bytes 1548292
  306.0 4.4 %copy-start.30 = (f32[144]{0:T(256)S(1)}, f32[144]{0:T(256)}, u32[]{:S(2)}) copy-start(f32[144]{0:T(256)} %get-tuple-element.59) | copy-start | bytes 1732

commit v4 on v3

--- a/solution.py
+++ b/solution.py
@@ -244,6 +244,9 @@
         compiler_params=pltpu.CompilerParams(
             collective_id=0, has_side_effects=True, vmem_limit_bytes=54 * 1024 * 1024
         ),
+        cost_estimate=pl.CostEstimate(
+            flops=0, bytes_accessed=200 * 1024 * 1024, transcendentals=0
+        ),
         name="replica_sum",
     )(*arrays)
 
@@ -331,16 +334,17 @@
     joined = jnp.concatenate([joined, line], axis=2).reshape(pairs, copies, lines, half)
     folded = [
         a.astype(jnp.bfloat16).reshape(copies, a.shape[0] // copies, a.shape[1])
-        for a in (gate, up, down)
+        for a in (up, down)
     ]
-    gate_s, up_s, down_s, joined = replica_sum([*folded, joined], copies)
+    gate_s = lax.psum(gate.astype(jnp.bfloat16), "replica")
+    up_s, down_s, joined = replica_sum([*folded, joined], copies)
     joined = joined.reshape(2, rows + lines, half)
     joined = jnp.concatenate([joined[0], joined[1]], axis=1)
     return (
         joined[rows, :share],
         joined[:rows, : qkv.shape[1]],
         joined[:rows, qkv.shape[1] :],
-        gate_s.reshape(gate.shape),
+        gate_s,
         up_s.reshape(up.shape),
         down_s.reshape(down.shape),
     )

time: 312 us -> 331 us (1.061)
  between operations: 1.41 us -> 14.8 us
  Pallas kernels: 193 us -> 187 us
  local copies, waits for them, and re-layouts: 15.9 us -> 20.4 us
  matrix products: 39.3 us -> 42.7 us
    pallas_call x1, Pallas kernels: 193 us -> 187 us  [replica_sum(): pl.pallas_call(functools.partial(sum_kernel, copies, tuple(pieces), swapp...]
    unnamed x86 -> x98, local copies, waits for them, and re-layouts: 4.33 us -> 6.72 us
  transfers between devices with their start and end apart: 9 -> 10, of which waited for: 5 -> 4; matrix products, arithmetic and copies ran while one was open for 9% -> 22% of each run, Pallas kernels for 0% -> 57%
where the time goes in v4:
time: 331 us
  Pallas kernels  187 us (56%)
  matrix products  42.7 us (13%)
  other arithmetic  34.2 us (10%)
  waiting for transfers between devices  22 us (7%)
  local copies, waits for them, and re-layouts  20.4 us (6%)
  between operations  14.8 us (4%)
  starting transfers between devices  9.28 us (3%)
    pallas_call x1, Pallas kernels, replica_sum(): pl.pallas_call(functools.partial(sum_kernel, copies, tuple(pieces), swapp...  187 us
    ppermute x7, waiting for transfers between devices, swap(): return lax.ppermute(values, 'group', [(0, 1), (1, 0)])  21.7 us
    dot_general x5, matrix products, outer_sum(): lax.dot_general(left, right, (((0,), (0,)), ((), ())), preferred_element_...  18.4 us
    convert_element_type x6, other arithmetic, on_device(): a.astype(jnp.float32)  17.8 us
    dot_general x5, matrix products, times_transposed(): lax.dot_general(left, right, (((1,), (1,)), ((), ())), preferred_element_...  11.4 us
    ppermute x7, starting transfers between devices, swap(): return lax.ppermute(values, 'group', [(0, 1), (1, 0)])  9.24 us
    dot_general x5, matrix products, matmul(): return jnp.dot(left, right, preferred_element_type=jnp.float32)  8.64 us
    unnamed x98, local copies, waits for them, and re-layouts  6.72 us
  transfers between devices with their start and end apart: 10, of which 4 were waited for; matrix products, arithmetic and copies ran while one was open for 22% of the time, Pallas kernels for 57%

profile of v4, /device:TPU:0, one launch (start us, length us, event | category | flops | bytes accessed | tf_op | source)
XLA Modules:
  0.0 330.8 jit_solution(7014947894428703526)
XLA Ops:
  7.2 2.2 concatenate.91
  9.4 3.0 collective-permute-start
  12.4 1.1 constant_dynamic-slice_fusion
  13.6 1.1 constant_dynamic-slice_fusion.1
  14.7 2.0 collective-permute-start.1
  16.8 1.0 select_reduce_fusion
  17.7 1.5 select_compare_fusion
  19.5 0.6 multiply_multiply_fusion
  20.3 5.5 %collective-permute-done.3 = bf16[224,896]{1,0:T(8,128)(2,1)S(1)} collective-permute-done((bf16[224,896]{1,0:T(8,128)(2,1)S(1)}, bf16[224,896]{1,0:T(8,128)(2,1)S(1)}, u32[]{:S(2)}, u32[]{:S(2)}) %collective-permute-start.3) | collective-permute-done | bytes 401440 | tf_op jit(solution)/shard_map/ppermute | solution.py:255
  26.2 9.2 %collective-permute-done.1 = bf16[224,1152]{1,0:T(8,128)(2,1)S(1)} collective-permute-done((bf16[224,1152]{1,0:T(8,128)(2,1)S(1)}, bf16[224,1152]{1,0:T(8,128)(2,1)S(1)}, u32[]{:S(2)}, u32[]{:S(2)}) %collective-permute-start.1) | collective-permute-done | bytes 516128 | tf_op jit(solution)/shard_map/ppermute | solution.py:255
  35.5 1.5 broadcast_select_fusion.3
  37.4 0.4 broadcast_select_fusion.1
  37.8 0.6 convolution_add_fusion
  39.9 0.6 subtract_convert_fusion
  40.5 0.5 copy.91
  40.9 0.5 copy.92
  41.4 1.3 fusion.61
  43.2 0.5 convolution_convert_fusion.5
  44.1 0.6 multiply_reduce_fusion.2
  44.8 0.6 multiply_multiply_fusion.1
  45.5 0.4 collective-permute-start.5
  45.9 1.7 collective-permute-start.7
  47.6 7.0 %collective-permute-done.5 = bf16[144,896]{1,0:T(8,128)(2,1)S(1)} collective-permute-done((bf16[144,896]{1,0:T(8,128)(2,1)S(1)}, bf16[144,896]{1,0:T(8,128)(2,1)S(1)}, u32[]{:S(2)}, u32[]{:S(2)}) %collective-permute-start.5) | collective-permute-done | bytes 258080 | tf_op jit(solution)/shard_map/ppermute | solution.py:255
  54.6 4.1 %fusion.53 = f32[288,2432]{1,0:T(8,128)S(1)} fusion(bf16[896,2432]{1,0:T(8,128)(2,1)} %param.19, bf16[144,896]{1,0:T(8,128)(2,1)S(1)} %collective-permute-done.5, bf16[144,896]{1,0:T(8,128)(2,1)S(1)} %multiply_convert_fusion.3), kind=kOutput, calls=%fused_computation.141 | convolution fusion | flops 1256177664 | bytes 7675904 | tf_op jit(solution)/shard_map/dot_general | solution.py:66
  58.7 1.7 fusion.54
  60.4 3.6 %multiply_convert_fusion = (bf16[288,2432]{1,0:T(8,128)(2,1)S(1)}, bf16[288,2432]{1,0:T(8,128)(2,1)S(1)}, bf16[288,2432]{1,0:T(8,128)(2,1)S(1)}) fusion(f32[288,2432]{1,0:T(8,128)S(1)} %fusion.54, f32[288,2432]{1,0:T(8,128)S(1)} %fusion.53, bf16[2432,896]{1,0:T(8,128)(2,1)S(1)} %bitcast.160, bf16[144,896]{1,0:T(8,128)(2,1)S(1)} %collective-permute-done.7, ...), kind=kOutput, calls=%fused_computation.10 | convolution fusion | flops 1266683904 | bytes 14680064 | tf_op jit(solution)/shard_map/dot_general | solution.py:76
  64.1 1.7 fusion.62
  65.8 1.0 copy-done.22
  66.7 0.7 slice.206
  67.8 1.7 fusion.63
  69.5 1.7 convolution_add_fusion.1
  71.3 1.1 copy-done.5
  72.3 0.7 slice.205
  73.0 1.7 collective-permute-start.8
  74.8 4.6 %convolution_convert_fusion = bf16[896,2432]{1,0:T(8,128)(2,1)} fusion(bf16[288,2432]{1,0:T(8,128)(2,1)S(1)} %get-tuple-element.21, bf16[144,896]{1,0:T(8,128)(2,1)S(1)} %collective-permute-done.5, bf16[144,896]{1,0:T(8,128)(2,1)S(1)} %multiply_convert_fusion.3), kind=kOutput, calls=%fused_computation.2 | convolution fusion | flops 1258356736 | bytes 6275072 | tf_op jit(solution)/shard_map/dot_general | solution.py:70
  79.4 6.3 %convolution_convert_fusion.1 = bf16[2432,896]{1,0:T(8,128)(2,1)} fusion(bf16[288,2432]{1,0:T(8,128)(2,1)} %copy-done.35, bf16[144,896]{1,0:T(8,128)(2,1)} %copy-done.34, bf16[144,896]{1,0:T(8,128)(2,1)} %bitcast.152), kind=kOutput, calls=%fused_computation.3 | convolution fusion | flops 1258356736 | bytes 6275072 | tf_op jit(solution)/shard_map/dot_general | solution.py:70
  85.7 4.6 %convolution_convert_fusion.2 = bf16[896,2432]{1,0:T(8,128)(2,1)} fusion(bf16[288,2432]{1,0:T(8,128)(2,1)S(1)} %copy-done.37, bf16[144,896]{1,0:T(8,128)(2,1)S(1)} %copy-done.33, bf16[144,896]{1,0:T(8,128)(2,1)S(1)} %multiply_convert_fusion.3), kind=kOutput, calls=%fused_computation.4 | convolution fusion | flops 1258356736 | bytes 6275072 | tf_op jit(solution)/shard_map/dot_general | solution.py:70
  90.6 0.5 copy-done.9
  91.0 2.1 subtract_add_fusion
  93.2 1.3 convolution_convert_fusion.6
  94.5 2.0 convolution_convert_fusion.4
  96.5 1.2 copy.125
  97.7 1.1 fusion.27
  98.8 0.6 fusion.3
  99.4 0.5 fusion.10
  99.9 0.4 copy-done.11
  100.5 0.5 convolution_bitcast_fusion
  101.6 0.9 fusion.57
  102.5 0.6 copy.127
  103.1 1.6 copy.126
  105.7 3.1 fusion.21
  108.9 0.9 convolution_convert_fusion.3
  110.3 1.9 fusion.56
  112.5 2.3 fusion.1
  114.8 187.3 %replica_sum.1 = (bf16[16,56,2432]{2,1,0:T(8,128)(2,1)}, bf16[16,152,896]{2,1,0:T(8,128)(2,1)}, bf16[16,64,1024]{2,1,0:T(8,128)(2,1)}) custom-call(bf16[16,56,2432]{2,1,0:T(8,128)(2,1)} %bitcast.134, bf16[16,152,896]{2,1,0:T(8,128)(2,1)} %bitcast.133, bf16[2,16,64,1024]{3,2,1,0:T(8,128)(2,1)} %bitcast.125), custom_call_target="tpu_custom_call" | custom-call | bytes 209715200 | tf_op jit(solution)/shard_map/replica_sum/pallas_call | solution.py:230
  302.1 1.7 fusion.55
  303.9 0.6 slice_reduce_fusion
  304.5 0.7 fusion.58
  305.2 1.4 fusion.11
  306.6 1.3 slice_convert_fusion
  307.9 1.0 fusion.18
  308.9 4.4 %bitcast_convert_fusion.1 = f32[896,2432]{1,0:T(8,128)} fusion(bf16[16,56,2432]{2,1,0:T(8,128)(2,1)S(1)} %bitcast.138), kind=kLoop, calls=%fused_computation.6 | loop fusion | flops 2179072 | bytes 13074432 | tf_op jit(solution)/shard_map/convert_element_type | solution.py:474
  313.3 4.4 %bitcast_convert_fusion = f32[2432,896]{1,0:T(8,128)} fusion(bf16[16,152,896]{2,1,0:T(8,128)(2,1)S(1)} %bitcast.136), kind=kLoop, calls=%fused_computation.5 | loop fusion | flops 2179072 | bytes 13074432 | tf_op jit(solution)/shard_map/convert_element_type | solution.py:474
  317.7 6.3 %convert_element_type.166 = f32[896,2432]{1,0:T(8,128)} convert(bf16[896,2432]{1,0:T(8,128)(2,1)} %all-reduce.4.cloned.1.call-done) | non-fusion elementwise | flops 2179072 | bytes 13074432 | tf_op jit(solution)/shard_map/convert_element_type | solution.py:474
  (157 shorter events, 7.2 us)
Async XLA Ops:
  7.2 12.0 %copy-start.1 = (bf16[1,144,896]{2,1,0:T(8,128)(2,1)S(1)}, bf16[1,144,896]{2,1,0:T(8,128)(2,1)}, u32[]{:S(2)}) copy-start(bf16[1,144,896]{2,1,0:T(8,128)(2,1)} %param.11) | copy-start | bytes 774148
  7.2 310.5 %all-reduce.4.cloned.1.call-start = ((), (), s32[]{:S(2)}) async-start(), calls=%async_computation | async-start | bytes 8716288 | tf_op jit(solution)/shard_map/psum | solution.py:339
  9.4 10.9 %collective-permute-start = (bf16[1472]{0:T(1024)(128)(2,1)S(1)}, bf16[1472]{0:T(1024)(128)(2,1)S(1)}, u32[]{:S(2)}, u32[]{:S(2)}) collective-permute-start(bf16[1472]{0:T(1024)(128)(2,1)S(1)} %concatenate.91), channel_id=1, source_target_pairs={{0,16},{16,0},{1,17},{17,1},{2,18},{18,2},{3,19},{19,3},{4,20},{20... | collective-permute-start | bytes 8840 | tf_op jit(solution)/shard_map/ppermute | solution.py:255
  12.4 23.1 %copy-start.4 = (bf16[448,896]{1,0:T(8,128)(2,1)S(1)}, bf16[448,896]{1,0:T(8,128)(2,1)}, u32[]{:S(2)}) copy-start(bf16[448,896]{1,0:T(8,128)(2,1)} %param.16) | copy-start | bytes 2408452
  13.5 12.3 %collective-permute-start.3 = (bf16[224,896]{1,0:T(8,128)(2,1)S(1)}, bf16[224,896]{1,0:T(8,128)(2,1)S(1)}, u32[]{:S(2)}, u32[]{:S(2)}) collective-permute-start(bf16[224,896]{1,0:T(8,128)(2,1)S(1)} %constant_dynamic-slice_fusion), channel_id=1, source_target_pairs={{0,16},{16,0},{1,17},{17,1},{2,18},{18,2},{3,19},{19,3},{4,20},{20... | collective-permute-start | bytes 1204232 | tf_op jit(solution)/shard_map/ppermute | solution.py:255
  14.7 20.7 %collective-permute-start.1 = (bf16[224,1152]{1,0:T(8,128)(2,1)S(1)}, bf16[224,1152]{1,0:T(8,128)(2,1)S(1)}, u32[]{:S(2)}, u32[]{:S(2)}) collective-permute-start(bf16[224,1152]{1,0:T(8,128)(2,1)S(1)} %constant_dynamic-slice_fusion.1), channel_id=1, source_target_pairs={{0,16},{16,0},{1,17},{17,1},{2,18},{18,2},{3,19},{19,3},{4,20},{20... | collective-permute-start | bytes 1548296 | tf_op jit(solution)/shard_map/ppermute | solution.py:255
  20.2 19.7 %copy-start.18 = (f32[144,32]{1,0:T(8,128)}, f32[144,32]{1,0:T(8,128)S(1)}, u32[]{:S(2)}) copy-start(f32[144,32]{1,0:T(8,128)S(1)} %copy.89) | copy-start | bytes 55300
  20.3 19.6 %copy-start.20 = (f32[144,32]{1,0:T(8,128)}, f32[144,32]{1,0:T(8,128)S(1)}, u32[]{:S(2)}) copy-start(f32[144,32]{1,0:T(8,128)S(1)} %copy.90) | copy-start | bytes 55300
  25.8 9.6 %collective-permute-start.4 = (bf16[224,896]{1,0:T(8,128)(2,1)S(1)}, bf16[224,896]{1,0:T(8,128)(2,1)S(1)}, u32[]{:S(2)}, u32[]{:S(2)}) collective-permute-start(bf16[224,896]{1,0:T(8,128)(2,1)S(1)} %collective-permute-done.3), channel_id=1, source_target_pairs={{0,1},{1,0},{2,3},{3,2},{4,5},{5,4},{6,7},{7,6},{8,9},{9,8},{10,11... | collective-permute-start | bytes 1204232 | tf_op jit(solution)/shard_map/ppermute | solution.py:264
  35.4 1.9 collective-permute-start.2
  35.5 1.9 copy-start
  37.8 1.0 copy-start.7
  37.8 1.3 copy-start.8
  39.5 1.9 copy-start.28
  40.9 2.2 copy-start.10
  41.4 1.7 copy-start.12
  42.8 1.1 copy-start.14
  42.8 1.4 copy-start.16
  43.6 1.8 copy-start.2
  44.1 1.7 copy-start.26
  45.5 9.1 %collective-permute-start.5 = (bf16[144,896]{1,0:T(8,128)(2,1)S(1)}, bf16[144,896]{1,0:T(8,128)(2,1)S(1)}, u32[]{:S(2)}, u32[]{:S(2)}) collective-permute-start(bf16[144,896]{1,0:T(8,128)(2,1)S(1)} %multiply_convert_fusion.3), channel_id=1, source_target_pairs={{0,16},{16,0},{1,17},{17,1},{2,18},{18,2},{3,19},{19,3},{4,20},{20... | collective-permute-start | bytes 774152 | tf_op jit(solution)/shard_map/ppermute | solution.py:255
  45.9 12.8 %slice-start.6 = ((s8[4358144]{0:T(1024)(128)(4,1)}), s8[4194304]{0:T(1024)(128)(4,1)S(1)}, s32[]{:S(2)}) async-start(s8[4358144]{0:T(1024)(128)(4,1)} %bitcast.161), calls=%async_computation.7 | async-start | bytes 8388608
  45.9 12.8 %slice-start.7 = ((s8[4358144]{0:T(1024)(128)(4,1)}), s8[163840]{0:T(1024)(128)(4,1)S(1)}, s32[]{:S(2)}) async-start(s8[4358144]{0:T(1024)(128)(4,1)} %bitcast.161), calls=%async_computation.8 | async-start | bytes 327680
  45.9 14.5 %collective-permute-start.7 = (bf16[144,896]{1,0:T(8,128)(2,1)S(1)}, bf16[144,896]{1,0:T(8,128)(2,1)S(1)}, u32[]{:S(2)}, u32[]{:S(2)}) collective-permute-start(bf16[144,896]{1,0:T(8,128)(2,1)S(1)} %bitcast.153), channel_id=1, source_target_pairs={{0,16},{16,0},{1,17},{17,1},{2,18},{18,2},{3,19},{19,3},{4,20},{20... | collective-permute-start | bytes 774152 | tf_op jit(solution)/shard_map/ppermute | solution.py:255
  54.6 20.2 %copy-start.32 = (bf16[144,896]{1,0:T(8,128)(2,1)}, bf16[144,896]{1,0:T(8,128)(2,1)S(1)}, u32[]{:S(2)}) copy-start(bf16[144,896]{1,0:T(8,128)(2,1)S(1)} %collective-permute-done.5) | copy-start | bytes 774148
  54.6 5.8 %slice-start.4 = ((s8[4358144]{0:T(1024)(128)(4,1)}), s8[4194304]{0:T(1024)(128)(4,1)S(1)}, s32[]{:S(2)}) async-start(s8[4358144]{0:T(1024)(128)(4,1)} %bitcast.159), calls=%async_computation.5 | async-start | bytes 8388608
  58.7 1.7 slice-start.5
  60.4 3.6 %copy-start.34 = (bf16[144,896]{1,0:T(8,128)(2,1)}, bf16[144,896]{1,0:T(8,128)(2,1)S(1)}, u32[]{:S(2)}) copy-start(bf16[144,896]{1,0:T(8,128)(2,1)S(1)} %collective-permute-done.7) | copy-start | bytes 774148
  64.0 1.7 copy-start.35
  64.0 5.4 %copy-start.36 = (bf16[288,2432]{1,0:T(8,128)(2,1)}, bf16[288,2432]{1,0:T(8,128)(2,1)S(1)}, u32[]{:S(2)}) copy-start(bf16[288,2432]{1,0:T(8,128)(2,1)S(1)} %get-tuple-element.20) | copy-start | bytes 4202500
  64.1 5.4 %slice-start.8 = ((s8[4358144]{0:T(1024)(128)(4,1)}), s8[4194304]{0:T(1024)(128)(4,1)S(1)}, s32[]{:S(2)}) async-start(s8[4358144]{0:T(1024)(128)(4,1)} %bitcast.163), calls=%async_computation.9 | async-start | bytes 8388608
  65.8 1.0 copy-start.22
  67.5 23.1 %collective-permute-start.6 = (bf16[144,896]{1,0:T(8,128)(2,1)}, bf16[144,896]{1,0:T(8,128)(2,1)}, u32[]{:S(2)}, u32[]{:S(2)}) collective-permute-start(bf16[144,896]{1,0:T(8,128)(2,1)} %slice.206), channel_id=1, source_target_pairs={{0,16},{16,0},{1,17},{17,1},{2,18},{18,2},{3,19},{19,3},{4,20},{20... | collective-permute-start | bytes 774152 | tf_op jit(solution)/shard_map/ppermute | solution.py:255
  67.8 1.7 slice-start.9
  71.2 1.1 copy-start.5
  73.0 17.3 %collective-permute-start.8 = (bf16[144,896]{1,0:T(8,128)(2,1)}, bf16[144,896]{1,0:T(8,128)(2,1)S(1)}, u32[]{:S(2)}, u32[]{:S(2)}) collective-permute-start(bf16[144,896]{1,0:T(8,128)(2,1)} %slice.205), channel_id=1, source_target_pairs={{0,16},{16,0},{1,17},{17,1},{2,18},{18,2},{3,19},{19,3},{4,20},{20... | collective-permute-start | bytes 774152 | tf_op jit(solution)/shard_map/ppermute | solution.py:255
  79.4 6.3 %copy-start.33 = (bf16[144,896]{1,0:T(8,128)(2,1)S(1)}, bf16[144,896]{1,0:T(8,128)(2,1)}, u32[]{:S(2)}) copy-start(bf16[144,896]{1,0:T(8,128)(2,1)} %copy-done.32) | copy-start | bytes 774148
  79.4 6.3 %copy-start.37 = (bf16[288,2432]{1,0:T(8,128)(2,1)S(1)}, bf16[288,2432]{1,0:T(8,128)(2,1)}, u32[]{:S(2)}) copy-start(bf16[288,2432]{1,0:T(8,128)(2,1)} %copy-done.36) | copy-start | bytes 4202500
  85.7 4.7 %copy-start.6 = (f32[288,896]{1,0:T(8,128)S(1)}, f32[288,896]{1,0:T(8,128)}, u32[]{:S(2)}) copy-start(f32[288,896]{1,0:T(8,128)} %copy-done.5) | copy-start | bytes 3096580
  85.7 5.4 %copy-start.23 = (f32[288,896]{1,0:T(8,128)S(1)}, f32[288,896]{1,0:T(8,128)}, u32[]{:S(2)}) copy-start(f32[288,896]{1,0:T(8,128)} %copy-done.22) | copy-start | bytes 3096580
  85.7 5.3 %copy-start.27 = (bf16[1,144,896]{2,1,0:T(8,128)(2,1)S(1)}, bf16[1,144,896]{2,1,0:T(8,128)(2,1)}, u32[]{:S(2)}) copy-start(bf16[1,144,896]{2,1,0:T(8,128)(2,1)} %param.21) | copy-start | bytes 774148
  85.7 5.3 %copy-start.31 = (f32[144]{0:T(256)S(1)}, f32[144]{0:T(256)}, u32[]{:S(2)}) copy-start(f32[144]{0:T(256)} %get-tuple-element.59) | copy-start | bytes 1732
  90.3 2.9 copy-start.15
  90.3 2.9 copy-start.17
  90.3 0.7 copy-start.9
  93.2 1.3 copy-start.3
  99.4 0.9 copy-start.11
  99.4 1.1 copy-start.13
  99.4 1.5 copy-start.29
  100.5 0.9 copy-start.24
  102.5 2.2 copy-start.19
  102.5 2.2 copy-start.21
  303.9 5.0 %slice-start.2 = ((s8[4358144]{0:T(1024)(128)(4,1)}), s8[4194304]{0:T(1024)(128)(4,1)S(1)}, s32[]{:S(2)}) async-start(s8[4358144]{0:T(1024)(128)(4,1)} %bitcast.137), calls=%async_computation.3 | async-start | bytes 8388608
  305.1 3.7 %slice-start.3 = ((s8[4358144]{0:T(1024)(128)(4,1)}), s8[163840]{0:T(1024)(128)(4,1)S(1)}, s32[]{:S(2)}) async-start(s8[4358144]{0:T(1024)(128)(4,1)} %bitcast.137), calls=%async_computation.4 | async-start | bytes 327680
  306.6 1.3 copy-start.25
  306.6 1.3 copy-start.30
  307.9 5.4 %slice-start = ((s8[4358144]{0:T(1024)(128)(4,1)}), s8[4194304]{0:T(1024)(128)(4,1)S(1)}, s32[]{:S(2)}) async-start(s8[4358144]{0:T(1024)(128)(4,1)} %bitcast.135), calls=%async_computation.1 | async-start | bytes 8388608
  308.9 4.4 %slice-start.1 = ((s8[4358144]{0:T(1024)(128)(4,1)}), s8[163840]{0:T(1024)(128)(4,1)S(1)}, s32[]{:S(2)}) async-start(s8[4358144]{0:T(1024)(128)(4,1)} %bitcast.135), calls=%async_computation.2 | async-start | bytes 327680
Sparse Core Ops, SparseCore 0:
  79.5 170.2 all-reduce.3
